TPU v7x, 256 devices: a whole 4x4x8 slice. The times are simulated.
256 devices in a mesh: ctx: 64 (over z, y, core), ch: 4 (over x).
Axes of the slice: x: 4, y: 4, z: 8, core: 2. Of those that a mesh axis runs over, the one named last changes fastest.
Arguments:
- features: bfloat16 [12288, 4096], P('ctx', 'ch'), may hold values from -6 to 6
- w_in: bfloat16 [4096, 3, 2048], P('ctx', None, 'ch'), may hold values from -0.09375 to 0.09375
- short_filter: float32 [3, 3, 2048], P(None, None, 'ch'), may hold values from -3 to 3
- filter_spectrum: float32 [2, 12288, 2048], P(None, 'ctx', 'ch'), may hold values from -6 to 6
- out_grad: bfloat16 [12288, 4096], P('ctx'), may hold values from -0.15625 to 0.15625
Outputs:
- gated: bfloat16 [12288, 2048], P('ctx', 'ch')
- w_out_grad: float32 [4096, 2048], P('ctx', 'ch')
All inputs are finite; a program needn't handle non-finite values.
Results may differ from a plain program's by a relative error of at most 0.0065.
Values may be sent and summed in bfloat16 or wider, within the bound.
A program may use at most 128 MiB of HBM per device.

v0:
```python
import math

import jax
import jax.numpy as jnp
from jax import lax
from jax.sharding import PartitionSpec as P

TWO_PI = 2.0 * math.pi


def from_behind(value, axis, by):
    count = lax.axis_size(axis)
    pairs = [(i, i + by) for i in range(count) if 0 <= i + by < count]
    return lax.ppermute(value, axis, pairs)


def partner(value, axis, stride):
    return lax.ppermute(value, axis, [(i, i ^ 1 << stride) for i in range(lax.axis_size(axis))])


def product(left, right):
    return jnp.dot(left, right, precision=lax.Precision.HIGHEST, preferred_element_type=jnp.float32)


def phase_tables(phase, period):
    angle = TWO_PI / period * phase.astype(jnp.float32)
    return (jnp.cos(angle), jnp.sin(angle))


def on_device(features, w_in, short_filter, filter_spectrum, out_grad):
    rows = features.shape[0]
    width = w_in.shape[2]
    devices = lax.axis_size("ctx")
    sections = devices.bit_length() - 1
    total = rows * devices
    place = lax.axis_index("ctx")
    whole = lax.all_gather(features, "ch", axis=1, tiled=True)
    flat_width = 3 * width
    piece = lax.all_gather(w_in, "ctx", axis=0, tiled=True)
    projected = jnp.dot(
        whole, piece.reshape(piece.shape[0], flat_width), preferred_element_type=jnp.float32
    )
    projected = projected.astype(jnp.bfloat16).reshape(rows, 3, width)
    earlier = from_behind(projected[rows - 2 :], "ctx", 1)
    extended = jnp.concatenate([earlier, projected], axis=0).astype(jnp.float32)
    mixed = (
        short_filter[0] * extended[2:]
        + short_filter[1] * extended[1 : rows + 1]
        + short_filter[2] * extended[:rows]
    )
    query = mixed[:, 0]
    signal = mixed[:, 1] * mixed[:, 2]
    local_pos = lax.broadcasted_iota(jnp.int32, (rows, 1), 0)
    grid = lax.broadcasted_iota(jnp.int32, (rows, rows), 0) * lax.broadcasted_iota(
        jnp.int32, (rows, rows), 1
    )
    local_cos, local_sin = phase_tables(grid % rows, rows)

    def twiddle(section):
        bit = sections - 1 - section
        offset = place % (1 << bit) * rows + local_pos
        return phase_tables(offset, total >> section)

    def high_side(bit):
        return place >> bit & 1 == 1

    first_bit = sections - 1
    other = partner(signal.astype(jnp.bfloat16), "ctx", first_bit).astype(signal.dtype)
    high = high_side(first_bit)
    wave_cos, wave_sin = twiddle(0)
    diff = other - signal
    real_part = jnp.where(high, diff * wave_cos, signal + other)
    imag_part = jnp.where(high, -diff * wave_sin, jnp.zeros_like(signal))
    data = jnp.stack([real_part, imag_part])
    for section in range(1, sections):
        bit = sections - 1 - section
        other = partner(data, "ctx", bit)
        high = high_side(bit)
        wave_cos, wave_sin = twiddle(section)
        diff = other - data
        rotated = jnp.stack(
            [diff[0] * wave_cos + diff[1] * wave_sin, diff[1] * wave_cos - diff[0] * wave_sin]
        )
        data = jnp.where(high, rotated, data + other)
    spec_real = product(local_cos, data[0]) + product(local_sin, data[1])
    spec_imag = product(local_cos, data[1]) - product(local_sin, data[0])
    prod_real = spec_real * filter_spectrum[0] - spec_imag * filter_spectrum[1]
    prod_imag = spec_real * filter_spectrum[1] + spec_imag * filter_spectrum[0]
    back_real = (product(local_cos, prod_real) - product(local_sin, prod_imag)) / rows
    back_imag = (product(local_cos, prod_imag) + product(local_sin, prod_real)) / rows
    data = jnp.stack([back_real, back_imag])
    for section in reversed(range(sections)):
        bit = sections - 1 - section
        other = partner(data, "ctx", bit)
        high = high_side(bit)
        wave_cos, wave_sin = twiddle(section)
        lower = jnp.where(high, other, data)
        upper = jnp.where(high, data, other)
        turned = jnp.stack(
            [upper[0] * wave_cos - upper[1] * wave_sin, upper[1] * wave_cos + upper[0] * wave_sin]
        )
        data = 0.5 * jnp.where(high, lower - turned, lower + turned)
    convolved = data[0]
    gated = (query * convolved).astype(jnp.bfloat16)
    w_out_grad = lax.psum_scatter(
        lax.dot_general(
            out_grad, gated, (((0,), (0,)), ((), ())), preferred_element_type=jnp.float32
        ),
        "ctx",
        scatter_dimension=0,
        tiled=True,
    )
    return (gated, w_out_grad)


def solution(mesh):
    in_specs = (
        P("ctx", "ch"),
        P("ctx", None, "ch"),
        P(None, None, "ch"),
        P(None, "ctx", "ch"),
        P("ctx", None),
    )
    out_specs = (P("ctx", "ch"), P("ctx", "ch"))
    return jax.shard_map(
        on_device, mesh=mesh, in_specs=in_specs, out_specs=out_specs, check_vma=False
    )
```

profile of v0, /device:TPU:1, one launch (start us, length us, event | category | flops | bytes accessed | tf_op | source)
XLA Modules:
  0.0 588.8 jit_solution(4127586449530294386)
XLA Ops:
  8.7 95.8 %all-gather.5.cloned.1.call-done = bf16[4096,3,512]{2,0,1:T(8,128)(2,1)} async-done(((bf16[64,3,512]{2,0,1:T(8,128)(2,1)}), bf16[4096,3,512]{2,0,1:T(8,128)(2,1)}) %all-gather.5.cloned.1.call-update) | async-done | bytes 12582928 | tf_op jit(solution)/shard_map/all_gather | solution.py:39
  104.5 17.0 %copy.14 = bf16[4096,3,512]{0,2,1:T(8,128)(2,1)} copy(bf16[4096,3,512]{2,0,1:T(8,128)(2,1)} %all-gather.5.cloned.1.call-done) | data formatting | bytes 25165824 | tf_op jit(solution)/shard_map/all_gather | solution.py:39
  121.5 10.2 %all-gather.3.cloned.1.call-done = bf16[192,4096]{1,0:T(8,128)(2,1)} async-done(((bf16[192,1024]{1,0:T(8,128)(2,1)}), bf16[192,4096]{1,0:T(8,128)(2,1)}) %all-gather.3.cloned.1.call-update) | async-done | bytes 1572880 | tf_op jit(solution)/shard_map/all_gather | solution.py:37
  131.7 9.3 %convolution_convert_fusion = bf16[192,1536]{1,0:T(8,128)(2,1)S(1)} fusion(bf16[192,4096]{1,0:T(8,128)(2,1)} %all-gather.3.cloned.1.call-done, bf16[4096,1536]{0,1:T(8,128)(2,1)} %bitcast.71), kind=kOutput, calls=%fused_computation.1 | convolution fusion | flops 2416214016 | bytes 14745600 | tf_op jit(solution)/shard_map/dot_general | solution.py:40
  141.1 3.8 collective-permute-start
  146.3 5.5 collective-permute-start.1
  151.8 3.1 collective-permute-done.1
  155.6 1.1 fusion.7
  156.7 1.0 pad_maximum_fusion
  157.7 4.7 collective-permute-start.2
  162.5 34.2 %collective-permute-done.2 = f32[2,192,512]{2,1,0:T(8,128)S(1)} collective-permute-done((f32[2,192,512]{2,1,0:T(8,128)}, f32[2,192,512]{2,1,0:T(8,128)S(1)}, u32[]{:S(2)}, u32[]{:S(2)}) %collective-permute-start.2) | collective-permute-done | bytes 786464 | tf_op jit(solution)/shard_map/ppermute | solution.py:18
  196.9 1.1 maximum_select_fusion
  198.1 18.0 %collective-permute-done.3 = f32[2,192,512]{2,1,0:T(8,128)} collective-permute-done((f32[2,192,512]{2,1,0:T(8,128)}, f32[2,192,512]{2,1,0:T(8,128)}, u32[]{:S(2)}, u32[]{:S(2)}) %collective-permute-start.3) | collective-permute-done | bytes 786464 | tf_op jit(solution)/shard_map/ppermute | solution.py:18
  216.1 1.6 fusion.102
  217.9 0.8 copy-done.3
  218.7 2.5 maximum_select_fusion.1
  221.2 5.5 collective-permute-start.4
  226.7 16.8 %collective-permute-done.4 = f32[2,192,512]{2,1,0:T(8,128)S(1)} collective-permute-done((f32[2,192,512]{2,1,0:T(8,128)}, f32[2,192,512]{2,1,0:T(8,128)S(1)}, u32[]{:S(2)}, u32[]{:S(2)}) %collective-permute-start.4) | collective-permute-done | bytes 786464 | tf_op jit(solution)/shard_map/ppermute | solution.py:18
  243.5 1.3 sub.94
  244.9 1.4 maximum_select_fusion.2
  246.3 2.2 collective-permute-start.5
  248.6 15.7 %collective-permute-done.5 = f32[2,192,512]{2,1,0:T(8,128)S(1)} collective-permute-done((f32[2,192,512]{2,1,0:T(8,128)S(1)}, f32[2,192,512]{2,1,0:T(8,128)S(1)}, u32[]{:S(2)}, u32[]{:S(2)}) %collective-permute-start.5) | collective-permute-done | bytes 786464 | tf_op jit(solution)/shard_map/ppermute | solution.py:18
  265.2 1.4 maximum_select_fusion.3
  266.6 3.0 collective-permute-start.6
  269.6 1.9 collective-permute-done.6
  272.1 1.3 fusion.14
  273.4 1.3 fusion.13
  274.7 1.3 convolution_add_fusion.1
  276.0 1.4 fusion.11
  277.3 1.3 fusion.23
  278.6 1.3 fusion.21
  279.9 1.3 fusion.1
  281.2 1.3 fusion.3
  283.0 1.9 collective-permute-done.7
  285.5 1.8 collective-permute-start.8
  287.3 17.3 %collective-permute-done.8 = f32[2,192,512]{2,1,0:T(8,128)S(1)} collective-permute-done((f32[2,192,512]{2,1,0:T(8,128)S(1)}, f32[2,192,512]{2,1,0:T(8,128)S(1)}, u32[]{:S(2)}, u32[]{:S(2)}) %collective-permute-start.8) | collective-permute-done | bytes 786464 | tf_op jit(solution)/shard_map/ppermute | solution.py:18
  305.6 2.5 collective-permute-start.9
  308.1 17.0 %collective-permute-done.9 = f32[2,192,512]{2,1,0:T(8,128)S(1)} collective-permute-done((f32[2,192,512]{2,1,0:T(8,128)S(1)}, f32[2,192,512]{2,1,0:T(8,128)S(1)}, u32[]{:S(2)}, u32[]{:S(2)}) %collective-permute-start.9) | collective-permute-done | bytes 786464 | tf_op jit(solution)/shard_map/ppermute | solution.py:18
  325.7 2.1 collective-permute-start.10
  327.7 16.1 %collective-permute-done.10 = f32[2,192,512]{2,1,0:T(8,128)S(1)} collective-permute-done((f32[2,192,512]{2,1,0:T(8,128)S(1)}, f32[2,192,512]{2,1,0:T(8,128)S(1)}, u32[]{:S(2)}, u32[]{:S(2)}) %collective-permute-start.10) | collective-permute-done | bytes 786464 | tf_op jit(solution)/shard_map/ppermute | solution.py:18
  344.4 3.4 collective-permute-start.11
  347.8 34.2 %collective-permute-done.11 = f32[2,192,512]{2,1,0:T(8,128)S(1)} collective-permute-done((f32[2,192,512]{2,1,0:T(8,128)S(1)}, f32[2,192,512]{2,1,0:T(8,128)S(1)}, u32[]{:S(2)}, u32[]{:S(2)}) %collective-permute-start.11) | collective-permute-done | bytes 786464 | tf_op jit(solution)/shard_map/ppermute | solution.py:18
  382.6 1.6 collective-permute-start.12
  384.2 37.0 %collective-permute-done.12 = f32[2,192,512]{2,1,0:T(8,128)S(1)} collective-permute-done((f32[2,192,512]{2,1,0:T(8,128)S(1)}, f32[2,192,512]{2,1,0:T(8,128)S(1)}, u32[]{:S(2)}, u32[]{:S(2)}) %collective-permute-start.12) | collective-permute-done | bytes 786464 | tf_op jit(solution)/shard_map/ppermute | solution.py:18
  421.5 1.2 fusion.10
  422.7 4.6 convolution_bitcast_fusion
  427.3 9.0 %copy.18 = f32[4096,512]{1,0:T(8,128)} copy(f32[4096,512]{0,1:T(8,128)} %convolution_bitcast_fusion) | data formatting | bytes 16777216
  436.3 146.0 %reduce-scatter.4.cloned.1.call-done = f32[64,512]{1,0:T(8,128)} async-done(((f32[4096,512]{1,0:T(8,128)}), f32[64,512]{1,0:T(8,128)}) %reduce-scatter.4.cloned.1.call-update) | async-done | bytes 131088
  (73 shorter events, 9.9 us)
Async XLA Ops:
  7.2 415.5 %copy-start = (bf16[192,4096]{1,0:T(8,128)(2,1)S(1)}, bf16[192,4096]{1,0:T(8,128)(2,1)}, u32[]{:S(2)}) copy-start(bf16[192,4096]{1,0:T(8,128)(2,1)} %param.9) | copy-start | bytes 4718596
  7.2 97.4 %all-gather.5.cloned.1.call-start = ((), (), s32[]{:S(2)}) async-start(), calls=%async_computation.2 | async-start | bytes 12779520 | tf_op jit(solution)/shard_map/all_gather | solution.py:39
  7.9 123.8 %all-gather.3.cloned.1.call-start = ((), (), s32[]{:S(2)}) async-start(), calls=%async_computation.1 | async-start | bytes 1966080 | tf_op jit(solution)/shard_map/all_gather | solution.py:37
  8.7 573.6 %reduce-scatter.4.cloned.1.call-start = ((), (), s32[]{:S(2)}) async-start(), calls=%async_computation.3 | async-start | bytes 8519680
  131.7 13.2 %copy-start.8 = (f32[3,3,512]{2,1,0:T(4,128)S(1)}, f32[3,3,512]{2,1,0:T(4,128)}, u32[]{:S(2)}) copy-start(f32[3,3,512]{2,1,0:T(4,128)} %param.7) | copy-start | bytes 55300
  141.1 4.6 collective-permute-start
  146.2 10.5 %copy-start.1 = (f32[192,3,512]{2,0,1:T(8,128)}, f32[192,3,512]{2,0,1:T(8,128)S(1)}, u32[]{:S(2)}) copy-start(f32[192,3,512]{2,0,1:T(8,128)S(1)} %fusion.4) | copy-start | bytes 3538948
  146.3 8.7 %collective-permute-start.1 = (bf16[192,512]{1,0:T(8,128)(2,1)S(1)}, bf16[192,512]{1,0:T(8,128)(2,1)S(1)}, u32[]{:S(2)}, u32[]{:S(2)}) collective-permute-start(bf16[192,512]{1,0:T(8,128)(2,1)S(1)} %fusion.92), channel_id=1, source_target_pairs={{0,128},{4,132},{8,136},{12,140},{16,144},{20,148},{24,152},{28,15... | collective-permute-start | bytes 589832 | tf_op jit(solution)/shard_map/ppermute | solution.py:18
  155.0 0.7 copy-start.7
  157.7 38.9 %collective-permute-start.2 = (f32[2,192,512]{2,1,0:T(8,128)}, f32[2,192,512]{2,1,0:T(8,128)S(1)}, u32[]{:S(2)}, u32[]{:S(2)}) collective-permute-start(f32[2,192,512]{2,1,0:T(8,128)} %pad_maximum_fusion), channel_id=1, source_target_pairs={{0,64},{4,68},{8,72},{12,76},{16,80},{20,84},{24,88},{28,92},{32,9... | collective-permute-start | bytes 2359304 | tf_op jit(solution)/shard_map/ppermute | solution.py:18
  196.9 1.2 copy-start.2
  198.1 18.1 %collective-permute-start.3 = (f32[2,192,512]{2,1,0:T(8,128)}, f32[2,192,512]{2,1,0:T(8,128)}, u32[]{:S(2)}, u32[]{:S(2)}) collective-permute-start(f32[2,192,512]{2,1,0:T(8,128)} %maximum_select_fusion), channel_id=1, source_target_pairs={{0,32},{4,36},{8,40},{12,44},{16,48},{20,52},{24,56},{28,60},{32,0... | collective-permute-start | bytes 2359304 | tf_op jit(solution)/shard_map/ppermute | solution.py:18
  198.1 19.6 %copy-start.9 = (f32[192]{0:T(256)}, f32[192]{0:T(256)S(1)}, u32[]{:S(2)}) copy-start(f32[192]{0:T(256)S(1)} %get-tuple-element.41) | copy-start | bytes 2308
  198.1 19.6 %copy-start.11 = (f32[192]{0:T(256)}, f32[192]{0:T(256)S(1)}, u32[]{:S(2)}) copy-start(f32[192]{0:T(256)S(1)} %get-tuple-element.42) | copy-start | bytes 2308
  217.7 1.0 copy-start.3
  221.2 22.3 %collective-permute-start.4 = (f32[2,192,512]{2,1,0:T(8,128)}, f32[2,192,512]{2,1,0:T(8,128)S(1)}, u32[]{:S(2)}, u32[]{:S(2)}) collective-permute-start(f32[2,192,512]{2,1,0:T(8,128)} %maximum_select_fusion.1), channel_id=1, source_target_pairs={{0,16},{4,20},{8,24},{12,28},{16,0},{20,4},{24,8},{28,12},{32,48},... | collective-permute-start | bytes 2359304 | tf_op jit(solution)/shard_map/ppermute | solution.py:18
  246.3 17.9 %collective-permute-start.5 = (f32[2,192,512]{2,1,0:T(8,128)S(1)}, f32[2,192,512]{2,1,0:T(8,128)S(1)}, u32[]{:S(2)}, u32[]{:S(2)}) collective-permute-start(f32[2,192,512]{2,1,0:T(8,128)S(1)} %maximum_select_fusion.2), channel_id=1, source_target_pairs={{0,8},{4,12},{8,0},{12,4},{16,24},{20,28},{24,16},{28,20},{32,40},... | collective-permute-start | bytes 2359304 | tf_op jit(solution)/shard_map/ppermute | solution.py:18
  264.3 0.9 copy-start.4
  266.6 4.9 collective-permute-start.6
  272.1 3.9 copy-start.6
  282.6 2.4 collective-permute-start.7
  285.5 19.0 %collective-permute-start.8 = (f32[2,192,512]{2,1,0:T(8,128)S(1)}, f32[2,192,512]{2,1,0:T(8,128)S(1)}, u32[]{:S(2)}, u32[]{:S(2)}) collective-permute-start(f32[2,192,512]{2,1,0:T(8,128)S(1)} %select_multiply_fusion.4), channel_id=1, source_target_pairs={{0,8},{4,12},{8,0},{12,4},{16,24},{20,28},{24,16},{28,20},{32,40},... | collective-permute-start | bytes 2359304 | tf_op jit(solution)/shard_map/ppermute | solution.py:18
  305.6 19.5 %collective-permute-start.9 = (f32[2,192,512]{2,1,0:T(8,128)S(1)}, f32[2,192,512]{2,1,0:T(8,128)S(1)}, u32[]{:S(2)}, u32[]{:S(2)}) collective-permute-start(f32[2,192,512]{2,1,0:T(8,128)S(1)} %select_multiply_fusion.3), channel_id=1, source_target_pairs={{0,16},{4,20},{8,24},{12,28},{16,0},{20,4},{24,8},{28,12},{32,48},... | collective-permute-start | bytes 2359304 | tf_op jit(solution)/shard_map/ppermute | solution.py:18
  325.6 18.3 %copy-start.10 = (f32[192]{0:T(256)S(1)}, f32[192]{0:T(256)}, u32[]{:S(2)}) copy-start(f32[192]{0:T(256)} %copy-done.9) | copy-start | bytes 2308
  325.7 18.3 %copy-start.12 = (f32[192]{0:T(256)S(1)}, f32[192]{0:T(256)}, u32[]{:S(2)}) copy-start(f32[192]{0:T(256)} %copy-done.11) | copy-start | bytes 2308
  325.7 18.2 %collective-permute-start.10 = (f32[2,192,512]{2,1,0:T(8,128)S(1)}, f32[2,192,512]{2,1,0:T(8,128)S(1)}, u32[]{:S(2)}, u32[]{:S(2)}) collective-permute-start(f32[2,192,512]{2,1,0:T(8,128)S(1)} %select_multiply_fusion.2), channel_id=1, source_target_pairs={{0,32},{4,36},{8,40},{12,44},{16,48},{20,52},{24,56},{28,60},{32,0... | collective-permute-start | bytes 2359304 | tf_op jit(solution)/shard_map/ppermute | solution.py:18
  344.4 37.6 %collective-permute-start.11 = (f32[2,192,512]{2,1,0:T(8,128)S(1)}, f32[2,192,512]{2,1,0:T(8,128)S(1)}, u32[]{:S(2)}, u32[]{:S(2)}) collective-permute-start(f32[2,192,512]{2,1,0:T(8,128)S(1)} %select_multiply_fusion.1), channel_id=1, source_target_pairs={{0,64},{4,68},{8,72},{12,76},{16,80},{20,84},{24,88},{28,92},{32,9... | collective-permute-start | bytes 2359304 | tf_op jit(solution)/shard_map/ppermute | solution.py:18
  382.6 38.5 %collective-permute-start.12 = (f32[2,192,512]{2,1,0:T(8,128)S(1)}, f32[2,192,512]{2,1,0:T(8,128)S(1)}, u32[]{:S(2)}, u32[]{:S(2)}) collective-permute-start(f32[2,192,512]{2,1,0:T(8,128)S(1)} %select_multiply_fusion), channel_id=1, source_target_pairs={{0,128},{4,132},{8,136},{12,140},{16,144},{20,148},{24,152},{28,15... | collective-permute-start | bytes 2359304 | tf_op jit(solution)/shard_map/ppermute | solution.py:18
  422.7 4.6 copy-start.5
Sparse Core Ops, SparseCore 0:
  10.8 93.6 all-gather.4
  106.3 25.2 all-gather.2
  436.4 145.7 reduce-scatter.3
where the time goes:
time: 593 us; the launch traced here: 589 us
  waiting for transfers between devices  467 us (79%)
  starting transfers between devices  36.7 us (6%)
  local copies, waits for them, and re-layouts  28.1 us (5%)
  matrix products  24.3 us (4%)
  other arithmetic  18.3 us (3%)
  between operations  14.2 us (2%)
    ppermute x12, waiting for transfers between devices, partner(): lax.ppermute(value, axis, [(i, i ^ 1 << stride) for i in range(lax.axis_s...  213 us
    unnamed x4, waiting for transfers between devices  147 us
    all_gather x1, waiting for transfers between devices, on_device(): piece = lax.all_gather(w_in, 'ctx', axis=0, tiled=True)  95.8 us
    ppermute x12, starting transfers between devices, partner(): lax.ppermute(value, axis, [(i, i ^ 1 << stride) for i in range(lax.axis_s...  32.7 us
    all_gather x1, local copies, waits for them, and re-layouts, on_device(): piece = lax.all_gather(w_in, 'ctx', axis=0, tiled=True)  17 us
  transfers between devices with their start and end apart: 16, of which 16 were waited for; matrix products, arithmetic and copies ran while one was open for 3% of the time, Pallas kernels for 0%

commit v1 on v0

v1 whole, which is shorter than its diff:
```python
import math

import jax
import jax.numpy as jnp
import numpy as np
from jax import lax
from jax.sharding import Mesh, PartitionSpec as P

CTX = ("z", "y", "core")
HIGH = lax.Precision.HIGHEST


def bit_reversed(count):
    bits = count.bit_length() - 1
    return np.array([int(format(i, f"0{bits}b")[::-1], 2) for i in range(count)])


def tables(shards, rows):
    total = shards * rows
    k1 = bit_reversed(shards)
    outer = 2 * np.pi / shards * np.outer(k1, np.arange(shards))
    turn = 2 * np.pi / total * np.outer(k1, np.arange(rows))
    inner = 2 * np.pi / rows * (np.outer(np.arange(rows), np.arange(rows)) % rows)
    f = lambda a: np.asarray(a, np.float32)
    return (
        f(np.concatenate([np.cos(outer), -np.sin(outer)])),
        f(np.cos(turn))[:, None, :],
        f(np.sin(turn))[:, None, :],
        f(np.block([[np.cos(inner), -np.sin(inner)], [np.sin(inner), np.cos(inner)]])),
    )


def on_device(features, w_in, short_filter, filter_spectrum, out_grad):
    rows = features.shape[0]
    width = w_in.shape[2]
    shards = lax.axis_size(CTX)
    zs = lax.axis_size("z")
    near = shards // zs
    total = rows * shards
    per = width // shards
    place = lax.axis_index(CTX)
    whole = lax.all_gather(features, "ch", axis=1, tiled=True)
    piece = lax.all_gather(w_in, CTX, axis=0, tiled=True)
    projected = jnp.dot(
        whole, piece.reshape(piece.shape[0], 3 * width), preferred_element_type=jnp.float32
    )
    projected = projected.astype(jnp.bfloat16).reshape(rows, 3, width)
    earlier = lax.ppermute(
        projected[rows - 2 :], CTX, [(i, i + 1) for i in range(shards - 1)]
    )
    extended = jnp.concatenate([earlier, projected], axis=0).astype(jnp.float32)
    mixed = (
        short_filter[0] * extended[2:]
        + short_filter[1] * extended[1 : rows + 1]
        + short_filter[2] * extended[:rows]
    )
    query = mixed[:, 0]
    signal = mixed[:, 1] * mixed[:, 2]

    outer, turn_cos, turn_sin, inner = tables(shards, rows)
    freq = filter_spectrum.astype(jnp.bfloat16).transpose(2, 0, 1).reshape(shards, per, 2, rows)
    freq = lax.all_to_all(freq, CTX, 0, 0, tiled=True).astype(jnp.float32)
    sent = signal.astype(jnp.bfloat16).T.reshape(shards, per * rows)
    data = lax.all_to_all(sent, CTX, 0, 0, tiled=True)
    data = jnp.dot(outer, data.astype(jnp.float32), precision=HIGH).reshape(2, shards, per, rows)
    turned = jnp.concatenate(
        [
            data[0] * turn_cos + data[1] * turn_sin,
            data[1] * turn_cos - data[0] * turn_sin,
        ],
        axis=-1,
    )
    spec = jnp.dot(turned, inner, precision=HIGH)
    spec_real, spec_imag = spec[..., :rows], spec[..., rows:]
    freq_real, freq_imag = freq[:, :, 0], freq[:, :, 1]
    prod = jnp.concatenate(
        [
            spec_real * freq_real - spec_imag * freq_imag,
            spec_real * freq_imag + spec_imag * freq_real,
        ],
        axis=-1,
    )
    back = lax.dot_general(prod, inner, (((2,), (1,)), ((), ())), precision=HIGH) / total
    back_real, back_imag = back[..., :rows], back[..., rows:]
    turned = jnp.concatenate(
        [
            back_real * turn_cos - back_imag * turn_sin,
            back_imag * turn_cos + back_real * turn_sin,
        ],
        axis=0,
    ).reshape(2 * shards, per * rows)
    convolved = jnp.dot(outer.T, turned, precision=HIGH).astype(jnp.bfloat16)
    convolved = lax.all_to_all(convolved, CTX, 0, 0, tiled=True)
    convolved = convolved.reshape(width, rows).T.astype(jnp.float32)
    gated = (query * convolved).astype(jnp.bfloat16)

    spread = out_grad.reshape(rows, zs, near, -1).transpose(2, 0, 1, 3).reshape(near, rows, -1)
    spread = lax.all_to_all(spread, ("y", "core"), 0, 0, tiled=True).reshape(near * rows, -1)
    column = lax.all_gather(gated, ("y", "core"), axis=0, tiled=True)
    w_out_grad = lax.psum_scatter(
        lax.dot_general(
            spread, column, (((0,), (0,)), ((), ())), preferred_element_type=jnp.float32
        ),
        "z",
        scatter_dimension=0,
        tiled=True,
    )
    return (gated, w_out_grad)


def solution(mesh):
    fine = Mesh(mesh.devices.reshape(8, 4, 2, 4), ("z", "y", "core", "ch"))
    in_specs = (
        P(CTX, "ch"),
        P(CTX, None, "ch"),
        P(None, None, "ch"),
        P(None, CTX, "ch"),
        P(CTX, None),
    )
    out_specs = (P(CTX, "ch"), P(CTX, "ch"))
    return jax.shard_map(
        on_device, mesh=fine, in_specs=in_specs, out_specs=out_specs, check_vma=False
    )
```

time: 593 us -> 286 us (0.48)
  waiting for transfers between devices: 467 us -> 137 us
  blocking collectives: 0 us -> 43.6 us
  other arithmetic: 18.3 us -> 8.95 us
  matrix products: 24.3 us -> 16.5 us
  starting transfers between devices: 36.7 us -> 29.4 us
    ppermute x13 -> x1, waiting for transfers between devices: 214 us -> 0.3 us  [on_device(): lax.ppermute(projected[rows - 2:], CTX, [(i, i + 1) for i in range(shards...]
    unnamed x4 -> x5, waiting for transfers between devices: 147 us -> 33.2 us
    all_to_all x0 -> x2, blocking collectives: none -> 43.6 us  [the longest x1 27.3 us: on_device(): lax.all_to_all(spread, ('y', 'core'), 0, 0, tiled=True)]
    ppermute x13 -> x1, starting transfers between devices: 36.6 us -> 3.84 us  [on_device(): lax.ppermute(projected[rows - 2:], CTX, [(i, i + 1) for i in range(shards...]
    all_to_all x0 -> x2, starting transfers between devices: none -> 25.2 us  [the longest x1 13.1 us: on_device(): freq = lax.all_to_all(freq, CTX, 0, 0, tiled=True).astype(jnp.float32)]
    all_gather x1 -> x2, waiting for transfers between devices: 95.8 us -> 82 us  [the longest x1 82 us: on_device(): piece = lax.all_gather(w_in, CTX, axis=0, tiled=True)]
    all_to_all x0 -> x2, waiting for transfers between devices: none -> 11.7 us  [the longest x1 11.7 us: on_device(): data = lax.all_to_all(sent, CTX, 0, 0, tiled=True)]
    dot_general x10 -> x6, matrix products: 24.3 us -> 16.5 us  [the longest x1 9.34 us: on_device(): jnp.dot(whole, piece.reshape(piece.shape[0], 3 * width), preferred_elemen...]
  transfers between devices with their start and end apart: 16 -> 7, of which waited for: 16 -> 5; matrix products, arithmetic and copies ran while one was open for 3% -> 15% of each run, Pallas kernels for 0% -> 0%
where the time goes in v1:
time: 286 us; the launch traced here: 281 us
  waiting for transfers between devices  137 us (48%)
  blocking collectives  43.6 us (15%)
  local copies, waits for them, and re-layouts  30.8 us (11%)
  starting transfers between devices  29.4 us (10%)
  matrix products  16.5 us (6%)
  between operations  14.1 us (5%)
  other arithmetic  8.95 us (3%)
    all_gather x1, waiting for transfers between devices, on_device(): piece = lax.all_gather(w_in, CTX, axis=0, tiled=True)  82 us
    unnamed x5, waiting for transfers between devices  33.2 us
    all_to_all x1, blocking collectives, on_device(): lax.all_to_all(spread, ('y', 'core'), 0, 0, tiled=True)  27.3 us
    all_gather x1, local copies, waits for them, and re-layouts, on_device(): piece = lax.all_gather(w_in, CTX, axis=0, tiled=True)  17 us
    all_to_all x1, blocking collectives, on_device(): convolved = lax.all_to_all(convolved, CTX, 0, 0, tiled=True)  16.3 us
    all_to_all x1, starting transfers between devices, on_device(): freq = lax.all_to_all(freq, CTX, 0, 0, tiled=True).astype(jnp.float32)  13.1 us
    all_to_all x1, starting transfers between devices, on_device(): data = lax.all_to_all(sent, CTX, 0, 0, tiled=True)  12.1 us
    all_to_all x1, waiting for transfers between devices, on_device(): data = lax.all_to_all(sent, CTX, 0, 0, tiled=True)  11.7 us
  transfers between devices with their start and end apart: 7, of which 5 were waited for; matrix products, arithmetic and copies ran while one was open for 15% of the time, Pallas kernels for 0%

profile of v1, /device:TPU:1, one launch (start us, length us, event | category | flops | bytes accessed | tf_op | source)
XLA Modules:
  0.0 280.7 jit_solution(14818106328226841699)
XLA Ops:
  7.2 0.7 all-gather.6.cloned.1.call-update
  7.9 0.7 all-gather.4.cloned.1.call-update
  8.6 1.2 convert_bitcast_fusion
  9.8 0.2 copy.61
  10.0 0.9 copy.62
  10.9 13.1 %all-to-all-start.1 = ((bf16[64,8,2,192]{3,1,2,0:T(8,128)(2,1)}), bf16[64,8,2,192]{3,1,2,0:T(8,128)(2,1)S(1)}, u32[]{:S(2)}, u32[]{:S(2)}) async-start(bf16[64,8,2,192]{3,1,2,0:T(8,128)(2,1)} %copy.62), calls=%async_computation.1 | async-start | bytes 1048576 | tf_op jit(solution)/shard_map/all_to_all | solution.py:62
  24.0 82.0 %all-gather.6.cloned.1.call-done = bf16[4096,3,512]{2,0,1:T(8,128)(2,1)} async-done(((bf16[64,3,512]{2,0,1:T(8,128)(2,1)}), bf16[4096,3,512]{2,0,1:T(8,128)(2,1)}) %all-gather.6.cloned.1.call-update) | async-done | bytes 12582928 | tf_op jit(solution)/shard_map/all_gather | solution.py:43
  106.1 17.0 %copy.58 = bf16[4096,3,512]{0,2,1:T(8,128)(2,1)} copy(bf16[4096,3,512]{2,0,1:T(8,128)(2,1)} %all-gather.6.cloned.1.call-done) | data formatting | bytes 25165824 | tf_op jit(solution)/shard_map/all_gather | solution.py:43
  123.1 10.1 %all-gather.4.cloned.1.call-done = bf16[192,4096]{1,0:T(8,128)(2,1)} async-done(((bf16[192,1024]{1,0:T(8,128)(2,1)}), bf16[192,4096]{1,0:T(8,128)(2,1)}) %all-gather.4.cloned.1.call-update) | async-done | bytes 1572880 | tf_op jit(solution)/shard_map/all_gather | solution.py:42
  133.2 9.3 %convolution_convert_fusion = bf16[192,1536]{1,0:T(8,128)(2,1)S(1)} fusion(bf16[192,4096]{1,0:T(8,128)(2,1)} %all-gather.4.cloned.1.call-done, bf16[4096,1536]{0,1:T(8,128)(2,1)} %bitcast.58), kind=kOutput, calls=%fused_computation | convolution fusion | flops 2416214016 | bytes 14745600 | tf_op jit(solution)/shard_map/dot_general | solution.py:44
  142.6 3.8 %collective-permute-start = (bf16[2,3,512]{2,1,0:T(4,128)(2,1)S(1)}, bf16[2,3,512]{2,1,0:T(4,128)(2,1)S(1)}, u32[]{:S(2)}, u32[]{:S(2)}) collective-permute-start(bf16[2,3,512]{2,1,0:T(4,128)(2,1)S(1)} %slice.63), channel_id=1, source_target_pairs={{0,4},{4,8},{8,12},{12,16},{16,20},{20,24},{24,28},{28,32},{32,36}... | collective-permute-start | bytes 18440 | tf_op jit(solution)/shard_map/ppermute | solution.py:48
  146.5 0.4 reshape.44
  146.9 0.3 collective-permute-done
  147.2 0.5 maximum_convert_fusion
  147.7 0.5 fusion.1
  148.2 0.8 fusion.10
  149.0 0.4 copy.76
  149.5 0.3 all_to_all.27
  149.8 0.5 broadcast.2
  150.3 1.8 reduce.2
  152.1 0.7 reshape.55
  152.9 12.1 %all-to-all-start = ((bf16[64,2,768]{2,1,0:T(2,128)(2,1)}), bf16[64,2,768]{2,1,0:T(2,128)(2,1)S(1)}, u32[]{:S(2)}, u32[]{:S(2)}) async-start(bf16[64,2,768]{2,1,0:T(2,128)(2,1)} %reshape.55), calls=%async_computation | async-start | bytes 393216 | tf_op jit(solution)/shard_map/all_to_all | solution.py:64
  164.9 0.2 all-gather.8.cloned.1.call-start
  165.3 11.7 %all-to-all-done = bf16[64,2,768]{2,1,0:T(2,128)(2,1)S(1)} async-done(((bf16[64,2,768]{2,1,0:T(2,128)(2,1)}), bf16[64,2,768]{2,1,0:T(2,128)(2,1)S(1)}, u32[]{:S(2)}, u32[]{:S(2)}) %all-to-all-start) | async-done | bytes 196640 | tf_op jit(solution)/shard_map/all_to_all | solution.py:64
  177.1 0.5 fusion.12
  177.8 0.2 squeeze.21
  178.0 0.4 copy-done.2
  178.4 1.0 multiply_add_fusion.2
  179.4 1.6 fusion.3
  181.0 0.3 multiply_subtract_fusion.1
  181.3 1.7 convolution_multiply_fusion
  183.0 0.3 multiply_subtract_fusion
  183.4 0.4 copy.64
  183.8 0.2 copy-done.5
  184.1 1.0 fusion
  185.1 0.7 reduce.3
  185.9 16.3 %all_to_all.32 = bf16[64,2,768]{2,1,0:T(2,128)(2,1)S(1)} all-to-all(bf16[64,2,768]{2,1,0:T(2,128)(2,1)S(1)} %reshape.57), channel_id=1, replica_groups=mesh['z'=8,'y'=4,'core'=2,'ch'=4] {'z','y','core'}, dimensions={0} | all-to-all | bytes 393216 | tf_op jit(solution)/shard_map/all_to_all | solution.py:93
  202.3 1.1 convert_reduce_fusion
  203.5 0.2 copy.66
  203.7 0.7 fusion.11
  204.5 0.3 copy-done.1
  204.8 2.5 copy.67
  207.3 1.7 copy.68
  209.0 2.3 copy.69
  211.3 27.3 %all_to_all.33 = bf16[8,192,512]{2,1,0:T(8,128)(2,1)S(1)} all-to-all(bf16[8,192,512]{2,1,0:T(8,128)(2,1)} %copy.69), channel_id=1, replica_groups=mesh['z'=8,'y'=4,'core'=2,'ch'=4] {'y','core'}, dimensions={0} | all-to-all | bytes 3145728 | tf_op jit(solution)/shard_map/all_to_all | solution.py:98
  238.6 2.4 convolution_bitcast_fusion
  241.0 1.3 copy.71
  242.4 31.8 %reduce-scatter.4.cloned.1.call-done = f32[64,512]{1,0:T(8,128)} async-done(((f32[512,512]{1,0:T(8,128)}), f32[64,512]{1,0:T(8,128)}) %reduce-scatter.4.cloned.1.call-update) | async-done | bytes 131088
  (29 shorter events, 1.1 us)
Async XLA Ops:
  7.2 98.9 %all-gather.6.cloned.1.call-start = ((), (), s32[]{:S(2)}) async-start(), calls=%async_computation.6 | async-start | bytes 12779520 | tf_op jit(solution)/shard_map/all_gather | solution.py:43
  7.9 125.3 %all-gather.4.cloned.1.call-start = ((), (), s32[]{:S(2)}) async-start(), calls=%async_computation.5 | async-start | bytes 1966080 | tf_op jit(solution)/shard_map/all_gather | solution.py:42
  10.9 142.0 %all-to-all-start.1 = ((bf16[64,8,2,192]{3,1,2,0:T(8,128)(2,1)}), bf16[64,8,2,192]{3,1,2,0:T(8,128)(2,1)S(1)}, u32[]{:S(2)}, u32[]{:S(2)}) async-start(bf16[64,8,2,192]{3,1,2,0:T(8,128)(2,1)} %copy.62), calls=%async_computation.1 | async-start | bytes 1048576 | tf_op jit(solution)/shard_map/all_to_all | solution.py:62
  133.2 13.2 %copy-start.6 = (f32[3,3,512]{2,1,0:T(4,128)S(1)}, f32[3,3,512]{2,1,0:T(4,128)}, u32[]{:S(2)}) copy-start(f32[3,3,512]{2,1,0:T(4,128)} %param.12) | copy-start | bytes 55300
  142.6 4.6 %collective-permute-start = (bf16[2,3,512]{2,1,0:T(4,128)(2,1)S(1)}, bf16[2,3,512]{2,1,0:T(4,128)(2,1)S(1)}, u32[]{:S(2)}, u32[]{:S(2)}) collective-permute-start(bf16[2,3,512]{2,1,0:T(4,128)(2,1)S(1)} %slice.63), channel_id=1, source_target_pairs={{0,4},{4,8},{8,12},{12,16},{16,20},{20,24},{24,28},{28,32},{32,36}... | collective-permute-start | bytes 18440 | tf_op jit(solution)/shard_map/ppermute | solution.py:48
  152.1 25.0 %copy-start.4 = (f32[128,64]{1,0:T(8,128)S(1)}, f32[128,64]{1,0:T(8,128)}, u32[]{:S(2)}) copy-start(f32[128,64]{1,0:T(8,128)} %constant.13.clone) | copy-start | bytes 98308
  152.9 24.1 %all-to-all-start = ((bf16[64,2,768]{2,1,0:T(2,128)(2,1)}), bf16[64,2,768]{2,1,0:T(2,128)(2,1)S(1)}, u32[]{:S(2)}, u32[]{:S(2)}) async-start(bf16[64,2,768]{2,1,0:T(2,128)(2,1)} %reshape.55), calls=%async_computation | async-start | bytes 393216 | tf_op jit(solution)/shard_map/all_to_all | solution.py:64
  164.9 73.7 %all-gather.8.cloned.1.call-start = ((), (), s32[]{:S(2)}) async-start(), calls=%async_computation.7 | async-start | bytes 1769472 | tf_op jit(solution)/shard_map/all_gather | solution.py:99
  177.6 0.8 copy-start.2
  177.8 1.6 copy-start
  181.3 1.7 copy-start.3
  183.3 0.8 copy-start.5
  203.3 1.5 copy-start.1
  204.5 69.7 %reduce-scatter.4.cloned.1.call-start = ((), (), s32[]{:S(2)}) async-start(), calls=%async_computation.8 | async-start | bytes 1179648
Sparse Core Ops, SparseCore 0:
  10.8 95.2 all-gather.5
  107.9 25.2 all-gather.3
  204.6 25.5 all-gather.7
  242.5 31.6 reduce-scatter.3

commit v2 on v1

--- a/solution.py
+++ b/solution.py
@@ -1,12 +1,19 @@
-import math
+import functools
+import heapq
 
 import jax
 import jax.numpy as jnp
 import numpy as np
 from jax import lax
+from jax.experimental import pallas as pl
+from jax.experimental.pallas import tpu as pltpu
 from jax.sharding import Mesh, PartitionSpec as P
 
 CTX = ("z", "y", "core")
+MESH = pl.DeviceIdType.MESH
+HALO = 16
+TILE = 256
+MATMUL_FROM = 36
 HIGH = lax.Precision.HIGHEST
 
 
@@ -30,6 +37,234 @@
     )
 
 
+def ring_plan(zs, ys, share):
+    z_max, z_min = zs // 2, -((zs - 1) // 2)
+    y_max, y_min = ys // 2, -((ys - 1) // 2)
+    size = {0: share * 2.1, 1: (1 - share) * 2.1}
+
+    def steps(at, low, high):
+        if at == 0:
+            return [d for d, ok in ((1, high > 0), (-1, low < 0)) if ok]
+        return [1] if 0 < at < high else [-1] if low < at < 0 else []
+
+    def onward(part, fz, fy):
+        along_z = [("z", d, (fz + d, fy)) for d in steps(fz, z_min, z_max)]
+        along_y = [("y", d, (fz, fy + d)) for d in steps(fy, y_min, y_max)]
+        if part == 0:
+            return (along_y if fz == 0 else []) + along_z
+        return (along_z if fy == 0 else []) + along_y
+
+    free = {"y": 0.0, "z": 0.0}
+    order, count = [], 2
+    waiting = [(0.0, 0, 1, 0, 0), (0.0, 1, 0, 0, 0)]
+    while waiting:
+        now, _, part, fz, fy = heapq.heappop(waiting)
+        sends = onward(part, fz, fy)
+        order.append((part, fz, fy, sends))
+        for axis, _, key in sends:
+            free[axis] = max(free[axis], now) + size[part]
+            count += 1
+            heapq.heappush(waiting, (free[axis] + 1.7, count, part, *key))
+    return order
+
+
+def project_kernel(
+    sizes, x_in, w_in, taps, query, signal, x_all, w_all, total,
+    local_sem, ring_send, ring_recv, twin_send, twin_recv, x_send, x_recv,
+    halo_send, halo_recv, edge_send, edge_recv,
+):
+    zs, ys, xs = sizes
+    rows, depth = x_in.shape
+    piece, flat = w_in.shape
+    width = flat // 3
+    first = 5 * flat // 12 // 128 * 128
+    z, y, core, x = (lax.axis_index(a) for a in ("z", "y", "core", "ch"))
+    turn = 1 - 2 * core
+    wrap = lambda v, n: lax.rem(v + 2 * n, n)
+    here = (z * ys + y) * 2 + core
+    shards = zs * ys * 2
+    after, before = lax.rem(here + 1, shards), lax.rem(here + shards - 1, shards)
+
+    def device(place):
+        return {"z": place // (2 * ys), "y": place // 2 % ys, "core": place % 2, "ch": x}
+
+    def by_axis(axis, step):
+        if axis == "z":
+            return {"z": wrap(z + turn * step, zs), "y": y, "core": core, "ch": x}
+        if axis == "y":
+            return {"z": z, "y": wrap(y + turn * step, ys), "core": core, "ch": x}
+        return {"z": z, "y": y, "core": core, "ch": lax.rem(x + step, xs)}
+
+    twin = {"z": z, "y": y, "core": 1 - core, "ch": x}
+    peers = [by_axis("z", 1), by_axis("z", -1), by_axis("y", 1), by_axis("y", -1), twin]
+    peers += [by_axis("ch", d) for d in range(1, xs)] + [device(after), device(before)]
+    barrier = pltpu.get_barrier_semaphore()
+    for peer in peers:
+        pl.semaphore_signal(barrier, inc=1, device_id=peer, device_id_type=MESH)
+    pl.semaphore_wait(barrier, len(peers))
+
+    def remote(src, dst, send, recv, to):
+        return pltpu.make_async_remote_copy(
+            src_ref=src, dst_ref=dst, send_sem=send, recv_sem=recv,
+            device_id=to, device_id_type=MESH,
+        )
+
+    sends = []
+
+    def start(copy):
+        copy.start()
+        sends.append(copy)
+
+    z_low, y_low = (zs - 1) // 2, (ys - 1) // 2
+    columns = (slice(0, first), slice(first, flat))
+
+    def slot(fz, fy, sign=1, of_core=None):
+        zo, yo = wrap(z - sign * turn * fz, zs), wrap(y - sign * turn * fy, ys)
+        which = (zo * ys + yo) * 2 + (core if of_core is None else of_core)
+        return pl.ds(pl.multiple_of(which * piece, piece), piece)
+
+    def ring_copy(part, origin, key, axis, step):
+        where = slot(*origin)
+        src = w_in.at[:, columns[part]] if origin == (0, 0) else w_all.at[where, columns[part]]
+        sem = (part, key[0] + z_low, key[1] + y_low)
+        return remote(
+            src, w_all.at[where, columns[part]], ring_send.at[sem], ring_recv.at[sem],
+            by_axis(axis, step),
+        )
+
+    def x_rows(of, n, row):
+        return x_all.at[pl.ds(row, n), pl.ds(pl.multiple_of(of * depth, depth), depth)]
+
+    plan = ring_plan(zs, ys, first / flat)
+    own_w = pltpu.make_async_copy(w_in, w_all.at[slot(0, 0)], local_sem.at[0])
+    own_x = pltpu.make_async_copy(x_in, x_rows(x, rows, HALO), local_sem.at[1])
+    start(remote(x_in.at[pl.ds(rows - HALO, HALO)], x_rows(x, HALO, 0), edge_send, edge_recv, device(after)))
+    arrived = set()
+    x_done = False
+    pending = []
+
+    def wait_x():
+        own_x.wait()
+        edge = remote(x_in.at[pl.ds(0, HALO)], x_rows(x, HALO, 0), edge_send, edge_recv, device(after))
+        edge.wait_recv()
+        for d in range(1, xs):
+            start(remote(x_rows(x, HALO, 0), x_rows(x, HALO, 0), halo_send.at[d - 1], halo_recv.at[d - 1], by_axis("ch", d)))
+
+    def wait_rest_of_x():
+        for d in range(1, xs):
+            of = lax.rem(x + xs - d, xs)
+            remote(x_in, x_rows(of, rows, HALO), x_send.at[d - 1], x_recv.at[d - 1], by_axis("ch", d)).wait_recv()
+        for d in range(1, xs):
+            of = lax.rem(x + xs - d, xs)
+            remote(x_rows(of, HALO, 0), x_rows(of, HALO, 0), halo_send.at[d - 1], halo_recv.at[d - 1], by_axis("ch", d)).wait_recv()
+
+    span = 2 * ys * piece
+
+    def mirror(f, n):
+        return f if 2 * f == n else -f
+
+    def multiply(fz, opening):
+        for fy in range(-y_low, ys // 2 + 1):
+            theirs = (mirror(fz, zs), mirror(fy, ys))
+            sem = (theirs[0] + z_low, theirs[1] + y_low)
+            where = slot(fz, fy, 1, 1 - core)
+            remote(w_all.at[where], w_all.at[where], twin_send.at[sem], twin_recv.at[sem], twin).wait_recv()
+        base = pl.multiple_of(wrap(z - turn * fz, zs) * span, span)
+        left = x_all[:, pl.ds(base, span)]
+
+        @pl.loop(0, flat // TILE)
+        def _(tile):
+            cols = pl.ds(pl.multiple_of(tile * TILE, TILE), TILE)
+            part = jnp.dot(left, w_all[pl.ds(base, span), cols], preferred_element_type=jnp.float32)
+            if opening:
+                total[:, cols] = part
+            else:
+                total[:, cols] += part
+
+    multiplied = []
+    for index, (part, fz, fy, onward) in enumerate(plan):
+        if (fz, fy) != (0, 0):
+            sem = (part, fz + z_low, fy + y_low)
+            where = slot(fz, fy)
+            remote(
+                w_all.at[where, columns[part]], w_all.at[where, columns[part]],
+                ring_send.at[sem], ring_recv.at[sem], twin,
+            ).wait_recv()
+        for axis, step, key in onward:
+            start(ring_copy(part, (fz, fy), key, axis, step))
+        arrived.add((part, fz, fy))
+        if (1 - part, fz, fy) in arrived:
+            sem = (fz + z_low, fy + y_low)
+            where = slot(fz, fy)
+            src = w_in if (fz, fy) == (0, 0) else w_all.at[where]
+            start(remote(src, w_all.at[where], twin_send.at[sem], twin_recv.at[sem], twin))
+        if index == 1:
+            own_w.start()
+            own_x.start()
+            for d in range(1, xs):
+                start(remote(x_in, x_rows(x, rows, HALO), x_send.at[d - 1], x_recv.at[d - 1], by_axis("ch", d)))
+        if index == 5:
+            wait_x()
+        ready = [k for k in range(-z_low, zs // 2 + 1) if k not in multiplied and k not in pending
+                 and all((p, g, f) in arrived for p in (0, 1) for g in (k, mirror(k, zs)) for f in range(-y_low, ys // 2 + 1))]
+        pending += sorted(ready, key=abs)
+        if pending and index >= MATMUL_FROM and index % 3 == 0:
+            if not multiplied:
+                own_w.wait()
+                wait_rest_of_x()
+            fz_now = pending.pop(0)
+            multiply(fz_now, not multiplied)
+            multiplied.append(fz_now)
+    for fz in pending:
+        multiply(fz, not multiplied)
+        multiplied.append(fz)
+    assert sorted(multiplied) == list(range(-z_low, zs // 2 + 1))
+
+    total[0:HALO] = jnp.where(here == 0, 0.0, total[0:HALO])
+    for at in range(0, width, TILE):
+        mixed = []
+        for j in range(3):
+            cols = slice(j * width + at, j * width + at + TILE)
+            mixed.append(sum(
+                taps[i : i + 1, cols]
+                * total[HALO - i : HALO - i + rows, cols].astype(jnp.bfloat16).astype(jnp.float32)
+                for i in range(3)
+            ))
+        query[:, at : at + TILE] = mixed[0]
+        signal[:, at : at + TILE] = (mixed[1] * mixed[2]).astype(jnp.bfloat16)
+    for copy in sends:
+        copy.wait_send()
+
+
+def project(features, w_in, short_filter, sizes):
+    zs, ys, xs = sizes
+    rows, depth = features.shape
+    piece, _, width = w_in.shape
+    flat = 3 * width
+    dma = pltpu.SemaphoreType.DMA
+    vmem = pl.BlockSpec(memory_space=pltpu.VMEM)
+    return pl.pallas_call(
+        functools.partial(project_kernel, sizes),
+        out_shape=(
+            jax.ShapeDtypeStruct((rows, width), jnp.float32),
+            jax.ShapeDtypeStruct((rows, width), jnp.bfloat16),
+        ),
+        in_specs=[vmem] * 3,
+        out_specs=(vmem, vmem),
+        scratch_shapes=[
+            pltpu.VMEM((rows + HALO, depth * xs), jnp.bfloat16),
+            pltpu.VMEM((piece * zs * ys * 2, flat), jnp.bfloat16),
+            pltpu.VMEM((rows + HALO, flat), jnp.float32),
+            dma((2,)), dma((2, zs, ys)), dma((2, zs, ys)), dma((zs, ys)), dma((zs, ys)),
+            dma((xs - 1,)), dma((xs - 1,)), dma((xs - 1,)), dma((xs - 1,)), dma, dma,
+        ],
+        compiler_params=pltpu.CompilerParams(
+            collective_id=0, has_side_effects=True, vmem_limit_bytes=48 << 20
+        ),
+        name="project",
+    )(features, w_in.reshape(piece, flat), short_filter.reshape(3, flat))
+
+
 def on_device(features, w_in, short_filter, filter_spectrum, out_grad):
     rows = features.shape[0]
     width = w_in.shape[2]
@@ -38,29 +273,13 @@
     near = shards // zs
     total = rows * shards
     per = width // shards
-    place = lax.axis_index(CTX)
-    whole = lax.all_gather(features, "ch", axis=1, tiled=True)
-    piece = lax.all_gather(w_in, CTX, axis=0, tiled=True)
-    projected = jnp.dot(
-        whole, piece.reshape(piece.shape[0], 3 * width), preferred_element_type=jnp.float32
-    )
-    projected = projected.astype(jnp.bfloat16).reshape(rows, 3, width)
-    earlier = lax.ppermute(
-        projected[rows - 2 :], CTX, [(i, i + 1) for i in range(shards - 1)]
-    )
-    extended = jnp.concatenate([earlier, projected], axis=0).astype(jnp.float32)
-    mixed = (
-        short_filter[0] * extended[2:]
-        + short_filter[1] * extended[1 : rows + 1]
-        + short_filter[2] * extended[:rows]
-    )
-    query = mixed[:, 0]
-    signal = mixed[:, 1] * mixed[:, 2]
+    sizes = tuple(lax.axis_size(a) for a in ("z", "y", "ch"))
+    query, signal = project(features, w_in, short_filter, sizes)
 
     outer, turn_cos, turn_sin, inner = tables(shards, rows)
     freq = filter_spectrum.astype(jnp.bfloat16).transpose(2, 0, 1).reshape(shards, per, 2, rows)
     freq = lax.all_to_all(freq, CTX, 0, 0, tiled=True).astype(jnp.float32)
-    sent = signal.astype(jnp.bfloat16).T.reshape(shards, per * rows)
+    sent = signal.T.reshape(shards, per * rows)
     data = lax.all_to_all(sent, CTX, 0, 0, tiled=True)
     data = jnp.dot(outer, data.astype(jnp.float32), precision=HIGH).reshape(2, shards, per, rows)
     turned = jnp.concatenate(

time: 286 us -> 215 us (0.75)
  the two profiles are of different devices: /device:TPU:1 before, /device:TPU:2 now
where the time goes in v2:
time: 215 us; the launch traced here: 214 us
  waiting for transfers between devices  61.8 us (29%)
  Pallas kernels  52.8 us (25%)
  blocking collectives  45.7 us (21%)
  local copies, waits for them, and re-layouts  16 us (7%)
  between operations  14.3 us (7%)
  starting transfers between devices  11.2 us (5%)
  matrix products  7.15 us (3%)
  other arithmetic  5.2 us (2%)
    pallas_call x1, Pallas kernels, project(): pl.pallas_call(functools.partial(project_kernel, sizes), out_shape=(jax.S...  52.8 us
    unnamed x3, waiting for transfers between devices  37.2 us
    all_to_all x1, blocking collectives, on_device(): lax.all_to_all(spread, ('y', 'core'), 0, 0, tiled=True)  28.2 us
    all_to_all x1, blocking collectives, on_device(): convolved = lax.all_to_all(convolved, CTX, 0, 0, tiled=True)  17.5 us
    all_to_all x1, waiting for transfers between devices, on_device(): freq = lax.all_to_all(freq, CTX, 0, 0, tiled=True).astype(jnp.float32)  13.8 us
    all_to_all x1, waiting for transfers between devices, on_device(): data = lax.all_to_all(sent, CTX, 0, 0, tiled=True)  10.8 us
    unnamed x23, local copies, waits for them, and re-layouts  7.94 us
    all_to_all x1, starting transfers between devices, on_device(): data = lax.all_to_all(sent, CTX, 0, 0, tiled=True)  6.31 us
  transfers between devices with their start and end apart: 4, of which 3 were waited for; matrix products, arithmetic and copies ran while one was open for 5% of the time, Pallas kernels for 0%

profile of v2, /device:TPU:2, one launch (start us, length us, event | category | flops | bytes accessed | tf_op | source)
XLA Modules:
  0.0 214.1 jit_solution(11907794964381586907)
XLA Ops:
  7.2 0.7 copy.73
  7.9 0.9 copy.72
  8.9 1.0 copy-done
  9.9 52.8 %project.1 = (f32[192,512]{1,0:T(8,128)S(1)}, bf16[192,512]{1,0:T(8,128)(2,1)S(1)}) custom-call(bf16[192,1024]{1,0:T(8,128)(2,1)S(1)} %copy-done, bf16[64,1536]{1,0:T(8,128)(2,1)S(1)} %bitcast.48, f32[3,1536]{1,0:T(4,128)S(1)} %bitcast.50), custom_call_target="tpu_custom_call" | custom-call | tf_op jit(solution)/shard_map/project/pallas_call | solution.py:246
  62.7 0.1 copy.57
  62.8 0.3 all_to_all.27
  63.1 0.5 broadcast.2
  63.7 1.8 reduce.2
  65.5 0.7 reshape.52
  66.2 6.3 %all-to-all-start = ((bf16[64,2,768]{2,1,0:T(2,128)(2,1)}), bf16[64,2,768]{2,1,0:T(2,128)(2,1)S(1)}, u32[]{:S(2)}, u32[]{:S(2)}) async-start(bf16[64,2,768]{2,1,0:T(2,128)(2,1)} %reshape.52), calls=%async_computation | async-start | bytes 393216 | tf_op jit(solution)/shard_map/all_to_all | solution.py:283
  72.6 0.2 copy.59
  72.8 0.8 copy.60
  73.6 10.8 %all-to-all-done = bf16[64,2,768]{2,1,0:T(2,128)(2,1)S(1)} async-done(((bf16[64,2,768]{2,1,0:T(2,128)(2,1)}), bf16[64,2,768]{2,1,0:T(2,128)(2,1)S(1)}, u32[]{:S(2)}, u32[]{:S(2)}) %all-to-all-start) | async-done | bytes 196640 | tf_op jit(solution)/shard_map/all_to_all | solution.py:283
  84.4 4.6 %all-to-all-start.1 = ((bf16[64,8,2,192]{3,1,2,0:T(8,128)(2,1)}), bf16[64,8,2,192]{3,1,2,0:T(8,128)(2,1)S(1)}, u32[]{:S(2)}, u32[]{:S(2)}) async-start(bf16[64,8,2,192]{3,1,2,0:T(8,128)(2,1)} %copy.60), calls=%async_computation.1 | async-start | bytes 1048576 | tf_op jit(solution)/shard_map/all_to_all | solution.py:281
  89.1 0.2 all-gather.2.cloned.1.call-start
  89.3 0.1 reshape.53
  89.5 0.5 fusion.9
  90.0 0.2 squeeze.15
  90.2 0.2 squeeze.14
  90.4 0.4 copy-done.4
  90.8 0.1 multiply_add_fusion.2
  90.9 0.3 copy-done.1
  91.3 1.6 fusion.1
  92.9 13.8 %all-to-all-done.1 = bf16[64,8,2,192]{3,1,2,0:T(8,128)(2,1)S(1)} async-done(((bf16[64,8,2,192]{3,1,2,0:T(8,128)(2,1)}), bf16[64,8,2,192]{3,1,2,0:T(8,128)(2,1)S(1)}, u32[]{:S(2)}, u32[]{:S(2)}) %all-to-all-start.1) | async-done | bytes 393248 | tf_op jit(solution)/shard_map/all_to_all | solution.py:281
  106.7 0.1 copy_convert_fusion
  106.8 0.3 multiply_subtract_fusion.1
  107.1 1.7 convolution_multiply_fusion
  108.8 0.3 multiply_subtract_fusion
  109.1 0.1 pad_maximum_fusion
  109.1 0.4 copy.62
  109.6 0.2 copy-done.7
  109.8 1.0 fusion
  110.8 0.7 reduce.3
  111.5 0.1 reshape.54
  111.6 17.5 %all_to_all.32 = bf16[64,2,768]{2,1,0:T(2,128)(2,1)S(1)} all-to-all(bf16[64,2,768]{2,1,0:T(2,128)(2,1)S(1)} %reshape.54), channel_id=1, replica_groups=mesh['z'=8,'y'=4,'core'=2,'ch'=4] {'z','y','core'}, dimensions={0} | all-to-all | bytes 393216 | tf_op jit(solution)/shard_map/all_to_all | solution.py:312
  129.1 0.1 reshape.55
  129.2 1.1 convert_reduce_fusion
  130.3 0.2 reshape.47
  130.5 0.2 copy.64
  130.7 0.7 fusion.8
  131.5 0.3 copy-done.2
  131.8 2.4 %copy.65 = bf16[192,4096]{0,1:T(8,128)(2,1)} copy(bf16[192,4096]{1,0:T(8,128)(2,1)S(1)} %copy-done.2) | data formatting | bytes 3145728 | tf_op args[4]
  134.2 1.7 copy.66
  135.9 2.3 %copy.67 = bf16[8,192,512]{2,1,0:T(8,128)(2,1)} copy(bf16[8,192,512]{1,2,0:T(8,128)(2,1)S(1)} %bitcast.51) | data formatting | bytes 3145728 | tf_op jit(solution)/shard_map/reshape | solution.py:316
  138.2 28.2 %all_to_all.33 = bf16[8,192,512]{2,1,0:T(8,128)(2,1)S(1)} all-to-all(bf16[8,192,512]{2,1,0:T(8,128)(2,1)} %copy.67), channel_id=1, replica_groups=mesh['z'=8,'y'=4,'core'=2,'ch'=4] {'y','core'}, dimensions={0} | all-to-all | bytes 3145728 | tf_op jit(solution)/shard_map/all_to_all | solution.py:317
  166.4 2.4 %convolution_bitcast_fusion = f32[512,512]{0,1:T(8,128)S(1)} fusion(bf16[1536,512]{1,0:T(8,128)(2,1)} %all-gather.2.cloned.1.call-done, bf16[1536,512]{1,0:T(8,128)(2,1)S(1)} %bitcast.53), kind=kOutput, calls=%fused_computation.2 | convolution fusion | flops 805306368 | bytes 4194304 | tf_op jit(solution)/shard_map/dot_general | solution.py:320
  168.9 1.3 copy.69
  170.2 37.1 %reduce-scatter.4.cloned.1.call-done = f32[64,512]{1,0:T(8,128)} async-done(((f32[512,512]{1,0:T(8,128)}), f32[64,512]{1,0:T(8,128)}) %reduce-scatter.4.cloned.1.call-update) | async-done | bytes 131088
  (17 shorter events, 0.3 us)
Async XLA Ops:
  8.9 1.0 copy-start
  9.9 62.6 %copy-start.3 = (f32[2,192,512]{2,1,0:T(8,128)S(1)}, f32[2,192,512]{2,1,0:T(8,128)}, u32[]{:S(2)}) copy-start(f32[2,192,512]{2,1,0:T(8,128)} %param.13) | copy-start | bytes 2359300
  66.2 18.3 %all-to-all-start = ((bf16[64,2,768]{2,1,0:T(2,128)(2,1)}), bf16[64,2,768]{2,1,0:T(2,128)(2,1)S(1)}, u32[]{:S(2)}, u32[]{:S(2)}) async-start(bf16[64,2,768]{2,1,0:T(2,128)(2,1)} %reshape.52), calls=%async_computation | async-start | bytes 393216 | tf_op jit(solution)/shard_map/all_to_all | solution.py:283
  72.8 16.7 %copy-start.6 = (f32[128,64]{1,0:T(8,128)S(1)}, f32[128,64]{1,0:T(8,128)}, u32[]{:S(2)}) copy-start(f32[128,64]{1,0:T(8,128)} %constant.13.clone) | copy-start | bytes 98308
  84.4 22.3 %all-to-all-start.1 = ((bf16[64,8,2,192]{3,1,2,0:T(8,128)(2,1)}), bf16[64,8,2,192]{3,1,2,0:T(8,128)(2,1)S(1)}, u32[]{:S(2)}, u32[]{:S(2)}) async-start(bf16[64,8,2,192]{3,1,2,0:T(8,128)(2,1)} %copy.60), calls=%async_computation.1 | async-start | bytes 1048576 | tf_op jit(solution)/shard_map/all_to_all | solution.py:281
  89.1 77.4 %all-gather.2.cloned.1.call-start = ((), (), s32[]{:S(2)}) async-start(), calls=%async_computation.5 | async-start | bytes 1769472 | tf_op jit(solution)/shard_map/all_gather | solution.py:318
  89.9 0.8 copy-start.4
  90.0 0.9 copy-start.5
  90.2 1.1 copy-start.1
  109.1 0.8 copy-start.7
  130.3 1.5 copy-start.2
  131.4 75.9 %reduce-scatter.4.cloned.1.call-start = ((), (), s32[]{:S(2)}) async-start(), calls=%async_computation.6 | async-start | bytes 1179648
Sparse Core Ops, SparseCore 0:
  131.5 26.3 all-gather.1
  170.3 36.9 reduce-scatter.3

commit v3 on v2

v3 whole, which is shorter than its diff:
```python
import functools
import heapq

import jax
import jax.numpy as jnp
import numpy as np
from jax import lax
from jax.experimental import pallas as pl
from jax.experimental.pallas import tpu as pltpu
from jax.sharding import Mesh, PartitionSpec as P

CTX = ("z", "y", "core")
MESH = pl.DeviceIdType.MESH
HALO = 16
TILE = 256
MATMUL_FROM = 36
F32 = jnp.float32
BF16 = jnp.bfloat16
HIGH = lax.Precision.HIGHEST


def ring_plan(zs, ys, share):
    z_max, z_min = zs // 2, -((zs - 1) // 2)
    y_max, y_min = ys // 2, -((ys - 1) // 2)
    size = {0: share * 2.1, 1: (1 - share) * 2.1}

    def steps(at, low, high):
        if at == 0:
            return [d for d, ok in ((1, high > 0), (-1, low < 0)) if ok]
        return [1] if 0 < at < high else [-1] if low < at < 0 else []

    def onward(part, fz, fy):
        along_z = [("z", d, (fz + d, fy)) for d in steps(fz, z_min, z_max)]
        along_y = [("y", d, (fz, fy + d)) for d in steps(fy, y_min, y_max)]
        if part == 0:
            return (along_y if fz == 0 else []) + along_z
        return (along_z if fy == 0 else []) + along_y

    free = {"y": 0.0, "z": 0.0}
    order, count = [], 2
    waiting = [(0.0, 0, 1, 0, 0), (0.0, 1, 0, 0, 0)]
    while waiting:
        now, _, part, fz, fy = heapq.heappop(waiting)
        sends = onward(part, fz, fy)
        order.append((part, fz, fy, sends))
        for axis, _, key in sends:
            free[axis] = max(free[axis], now) + size[part]
            count += 1
            heapq.heappush(waiting, (free[axis] + 1.7, count, part, *key))
    return order


def bit_reversed(count):
    bits = count.bit_length() - 1
    return np.array([int(format(i, f"0{bits}b")[::-1], 2) for i in range(count)])


def halves(table):
    high = table.astype(BF16)
    return high, (table - high.astype(np.float64)).astype(BF16)


def tables(shards, rows, per):
    total = shards * rows
    k1 = bit_reversed(shards)
    outer = 2 * np.pi / shards * (np.outer(k1, np.arange(shards)) % shards)
    turn = 2 * np.pi / total * np.outer(k1, np.arange(rows))
    turn = np.tile(np.repeat(turn, per // 2, axis=0), (1, 2))
    inner = 2 * np.pi / rows * (np.outer(np.arange(rows), np.arange(rows)) % rows)
    across = np.kron(np.concatenate([np.cos(outer), -np.sin(outer)]), np.eye(per // 2))
    pair = np.eye(2)
    return (
        *halves(across),
        np.cos(turn).astype(np.float32),
        np.sin(turn).astype(np.float32),
        *halves(np.kron(pair, np.cos(inner))),
        *halves(np.kron(pair, np.sin(inner))),
    )


def operator_kernel(
    sizes,
    x_in, w_in, taps, freq_hbm, grad_hbm,
    across_hi, across_lo, turn_cos, turn_sin, cos_hi, cos_lo, sin_hi, sin_lo,
    gated, w_grad,
    x_all, w_all, total, query, freq_in, freq_out, freq_all, grad_all,
    sig_out, sig_all, conv_out, conv_all, gated_all, part_out, part_all,
    local_sem, ring_send, ring_recv, twin_send, twin_recv, x_send, x_recv,
    halo_send, halo_recv, edge_send, edge_recv, freq_send, freq_recv,
    grad_send, grad_recv, grad_x_send, grad_x_recv, sig_send, sig_recv,
    conv_send, conv_recv, gated_send, gated_recv, part_send, part_recv,
):
    zs, ys, xs = sizes
    rows, depth = x_in.shape
    piece, flat = w_in.shape
    width = flat // 3
    half = width // 2
    shards = zs * ys * 2
    near = ys * 2
    first = 5 * flat // 12 // 128 * 128
    z, y, core, x = (lax.axis_index(a) for a in ("z", "y", "core", "ch"))
    turn = 1 - 2 * core
    wrap = lambda v, n: lax.rem(v + 2 * n, n)
    here = (z * ys + y) * 2 + core
    group = y * 2 + core

    def device(place):
        return {"z": place // near, "y": place // 2 % ys, "core": place % 2, "ch": x}

    def by_axis(axis, step):
        if axis == "z":
            return {"z": wrap(z + turn * step, zs), "y": y, "core": core, "ch": x}
        if axis == "y":
            return {"z": z, "y": wrap(y + turn * step, ys), "core": core, "ch": x}
        return {"z": z, "y": y, "core": core, "ch": lax.rem(x + step, xs)}

    def in_group(other):
        return {"z": z, "y": other // 2, "core": other % 2, "ch": x}

    twin = in_group(y * 2 + 1 - core)
    after, before = lax.rem(here + 1, shards), lax.rem(here + shards - 1, shards)
    peers = [by_axis("z", 1), by_axis("z", -1)]
    peers += [in_group(lax.rem(group + p, near)) for p in range(1, near)]
    peers += [by_axis("ch", d) for d in range(1, xs)] + [device(after), device(before)]
    barrier = pltpu.get_barrier_semaphore()
    for peer in peers:
        pl.semaphore_signal(barrier, inc=1, device_id=peer, device_id_type=MESH)
    pl.semaphore_wait(barrier, len(peers))

    def remote(src, dst, send, recv, to=twin):
        return pltpu.make_async_remote_copy(
            src_ref=src, dst_ref=dst, send_sem=send, recv_sem=recv,
            device_id=to, device_id_type=MESH,
        )

    sends = []

    def start(copy):
        copy.start()
        sends.append(copy)

    z_low, y_low = (zs - 1) // 2, (ys - 1) // 2
    columns = (slice(0, first), slice(first, flat))

    def place_of(fz, fy, of_core):
        zo, yo = wrap(z - turn * fz, zs), wrap(y - turn * fy, ys)
        return (zo * ys + yo) * 2 + of_core

    def slot(fz, fy, of_core):
        return pl.ds(pl.multiple_of(place_of(fz, fy, of_core) * piece, piece), piece)

    def ring_copy(part, origin, key, axis, step):
        where = slot(*origin, core)
        src = w_in.at[:, columns[part]] if origin == (0, 0) else w_all.at[where, columns[part]]
        sem = (part, key[0] + z_low, key[1] + y_low)
        return remote(
            src, w_all.at[where, columns[part]], ring_send.at[sem], ring_recv.at[sem],
            by_axis(axis, step),
        )

    def x_rows(of, n, row):
        return x_all.at[pl.ds(row, n), pl.ds(pl.multiple_of(of * depth, depth), depth)]

    def send_freq(place):
        remote(freq_out.at[place], freq_all.at[here], freq_send, freq_recv, device(place)).start()

    plan = ring_plan(zs, ys, first / flat)
    own_w = pltpu.make_async_copy(w_in, w_all.at[slot(0, 0, core)], local_sem.at[0])
    own_x = pltpu.make_async_copy(x_in, x_rows(x, rows, HALO), local_sem.at[1])
    load_freq = pltpu.make_async_copy(freq_hbm, freq_in, local_sem.at[2])

    share = rows // xs
    mine = pl.ds(pl.multiple_of(share * x, share), share)
    blocks = zs // 2

    def grad_piece(other, k):
        column = ((other % 2 * blocks + k) * ys + other // 2) * 128
        return grad_hbm.at[mine, pl.ds(pl.multiple_of(column, 128), 128)]

    own_grad = [
        pltpu.make_async_copy(
            grad_piece(group, k), grad_all.at[group, mine, pl.ds(128 * k, 128)], local_sem.at[3 + k]
        )
        for k in range(blocks)
    ]

    def open_x():
        own_w.start()
        own_x.start()
        load_freq.start()
        for d in range(1, xs):
            start(remote(x_in, x_rows(x, rows, HALO), x_send.at[d - 1], x_recv.at[d - 1], by_axis("ch", d)))
        for copy in own_grad:
            copy.start()
        for p in range(1, near):
            other = lax.rem(group + p, near)
            for k in range(blocks):
                remote(
                    grad_piece(other, k), grad_all.at[group, mine, pl.ds(128 * k, 128)],
                    grad_send, grad_recv, in_group(other),
                ).start()

    def pass_halo():
        own_x.wait()
        remote(x_in.at[pl.ds(0, HALO)], x_rows(x, HALO, 0), edge_send, edge_recv).wait_recv()
        for d in range(1, xs):
            start(remote(x_rows(x, HALO, 0), x_rows(x, HALO, 0), halo_send.at[d - 1], halo_recv.at[d - 1], by_axis("ch", d)))

    def turn_freq():
        load_freq.wait()
        for p in range(2):
            stacked = jnp.concatenate([freq_in[p, :, 0:half], freq_in[p, :, half:width]], axis=0)
            freq_out[:, p] = stacked.T.astype(BF16).reshape(shards, 4, 2 * rows)
        freq_all[here] = freq_out[here]

    grad_arrivals = lambda: grad_all.at[pl.ds(0, near - 1), pl.ds(0, share)]

    def close_x():
        own_w.wait()
        for d in range(1, xs):
            of = lax.rem(x + xs - d, xs)
            remote(x_in, x_rows(of, rows, HALO), x_send.at[d - 1], x_recv.at[d - 1]).wait_recv()
        for d in range(1, xs):
            of = lax.rem(x + xs - d, xs)
            remote(x_rows(of, HALO, 0), x_rows(of, HALO, 0), halo_send.at[d - 1], halo_recv.at[d - 1]).wait_recv()
        for copy in own_grad:
            copy.wait()
        remote(grad_arrivals(), grad_arrivals(), grad_send, grad_recv).wait_recv()
        for d in range(1, xs):
            start(remote(
                grad_all.at[:, mine], grad_all.at[:, mine],
                grad_x_send.at[d - 1], grad_x_recv.at[d - 1], by_axis("ch", d),
            ))

    def finish_grad():
        for d in range(1, xs):
            of = lax.rem(x + xs - d, xs)
            theirs = grad_all.at[:, pl.ds(pl.multiple_of(share * of, share), share)]
            remote(theirs, theirs, grad_x_send.at[d - 1], grad_x_recv.at[d - 1]).wait_recv()

    span = near * piece

    def mirror(f, n):
        return f if 2 * f == n else -f

    def multiply(fz, opening):
        for fy in range(-y_low, ys // 2 + 1):
            sem = (mirror(fz, zs) + z_low, mirror(fy, ys) + y_low)
            where = slot(fz, fy, 1 - core)
            remote(w_all.at[where], w_all.at[where], twin_send.at[sem], twin_recv.at[sem]).wait_recv()
            send_freq(place_of(fz, fy, 1 - core))
        base = pl.multiple_of(wrap(z - turn * fz, zs) * span, span)
        left = x_all[:, pl.ds(base, span)]

        @pl.loop(0, flat // TILE)
        def _(tile):
            cols = pl.ds(pl.multiple_of(tile * TILE, TILE), TILE)
            part = jnp.dot(left, w_all[pl.ds(base, span), cols], preferred_element_type=F32)
            if opening:
                total[:, cols] = part
            else:
                total[:, cols] += part

    start(remote(x_in.at[pl.ds(rows - HALO, HALO)], x_rows(x, HALO, 0), edge_send, edge_recv, device(after)))
    arrived, pending, multiplied = set(), [], []
    turned = False
    for index, (part, fz, fy, onward) in enumerate(plan):
        where = slot(fz, fy, core)
        if (fz, fy) != (0, 0):
            sem = (part, fz + z_low, fy + y_low)
            piece_at = w_all.at[where, columns[part]]
            remote(piece_at, piece_at, ring_send.at[sem], ring_recv.at[sem]).wait_recv()
        for axis, step, key in onward:
            start(ring_copy(part, (fz, fy), key, axis, step))
        arrived.add((part, fz, fy))
        if (1 - part, fz, fy) in arrived:
            sem = (fz + z_low, fy + y_low)
            src = w_in if (fz, fy) == (0, 0) else w_all.at[where]
            start(remote(src, w_all.at[where], twin_send.at[sem], twin_recv.at[sem], twin))
        if index == 1:
            open_x()
        if index == 5:
            pass_halo()
        if index == 11:
            turn_freq()
            turned = True
            for part_, fz_, fy_ in arrived_in_order(plan, index):
                send_freq(place_of(fz_, fy_, core))
        elif turned and (1 - part, fz, fy) in arrived:
            send_freq(place_of(fz, fy, core))
        pending += sorted(
            (k for k in range(-z_low, zs // 2 + 1) if k not in multiplied and k not in pending
             and all((p, g, f) in arrived for p in (0, 1) for g in (k, mirror(k, zs))
                     for f in range(-y_low, ys // 2 + 1))),
            key=abs,
        )
        if pending and index >= MATMUL_FROM and index % 3 == 0:
            if not multiplied:
                close_x()
            multiplied.append(pending.pop(0))
            multiply(multiplied[-1], len(multiplied) == 1)
    for fz in pending:
        multiply(fz, False)

    total[0:HALO] = jnp.where(here == 0, 0.0, total[0:HALO])

    def short(j, at):
        cols = slice(j * width + at, j * width + at + half)
        return sum(
            taps[i : i + 1, cols]
            * total[HALO - i : HALO - i + rows, cols].astype(BF16).astype(F32)
            for i in range(3)
        )

    signal = jnp.concatenate([short(1, at) * short(2, at) for at in (0, half)], axis=0)
    sig_out[...] = signal.T.astype(BF16).reshape(shards, 4, 2 * rows)

    def exchange(out, into, send, recv):
        @pl.loop(1, shards)
        def _(d):
            to = lax.rem(here + d, shards)
            remote(out.at[to], into.at[here], send, recv, device(to)).start()

        into[here] = out[here]

    others = pl.ds(0, shards - 1)

    def arrivals(into, send, recv):
        remote(into.at[others], into.at[others], send, recv).wait_recv()

    exchange(sig_out, sig_all, sig_send, sig_recv)
    for at in (0, half):
        query[:, at : at + half] = short(0, at)
    arrivals(freq_all, freq_send, freq_recv)
    arrivals(sig_all, sig_send, sig_recv)

    lines = 4 * shards
    mul = functools.partial(jnp.dot, preferred_element_type=F32)

    def split(value):
        high = value.astype(BF16)
        return high, (value - high.astype(F32)).astype(BF16)

    def within(real, imag):
        high, low = split(jnp.concatenate([real, imag], axis=0))
        cos = mul(high, cos_hi[...]) + mul(low, cos_hi[...]) + mul(high, cos_lo[...])
        sin = mul(high, sin_hi[...]) + mul(low, sin_hi[...]) + mul(high, sin_lo[...])
        return cos[:lines], cos[lines:], sin[:lines], sin[lines:]

    data = sig_all[...].reshape(lines, 2 * rows)
    data = mul(across_hi[...], data) + mul(across_lo[...], data)
    real, imag = data[:lines], data[lines:]
    real_cos, imag_cos, real_sin, imag_sin = within(
        real * turn_cos[...] + imag * turn_sin[...], imag * turn_cos[...] - real * turn_sin[...]
    )
    real, imag = real_cos + imag_sin, imag_cos - real_sin
    freq_real = freq_all[:, 0].reshape(lines, 2 * rows).astype(F32)
    freq_imag = freq_all[:, 1].reshape(lines, 2 * rows).astype(F32)
    real_cos, imag_cos, real_sin, imag_sin = within(
        real * freq_real - imag * freq_imag, real * freq_imag + imag * freq_real
    )
    real, imag = real_cos - imag_sin, imag_cos + real_sin
    high, low = split(jnp.concatenate(
        [real * turn_cos[...] - imag * turn_sin[...], imag * turn_cos[...] + real * turn_sin[...]],
        axis=0,
    ))
    back = lambda a, b: lax.dot_general(a, b, (((0,), (0,)), ((), ())), preferred_element_type=F32)
    data = back(across_hi[...], high) + back(across_hi[...], low) + back(across_lo[...], high)
    conv_out[...] = (data * (1 / (shards * rows))).astype(BF16).reshape(shards, 4, 2 * rows)
    exchange(conv_out, conv_all, conv_send, conv_recv)
    finish_grad()
    arrivals(conv_all, conv_send, conv_recv)

    conv = conv_all[...].reshape(lines, 2 * rows).astype(F32).T
    for n, at in enumerate((0, half)):
        value = (query[:, at : at + half] * conv[n * rows : (n + 1) * rows]).astype(BF16)
        gated_all[group, :, at : at + half] = value
    for p in range(1, near):
        start(remote(
            gated_all.at[group], gated_all.at[group], gated_send.at[p - 1], gated_recv.at[p - 1],
            in_group(lax.rem(group + p, near)),
        ))
    gated[...] = gated_all[group]
    for p in range(1, near):
        theirs = gated_all.at[lax.rem(group + near - p, near)]
        remote(theirs, theirs, gated_send.at[p - 1], gated_recv.at[p - 1]).wait_recv()
    right = gated_all[...].reshape(near * rows, width)
    count = part_out.shape[1]
    for k in range(blocks):
        left = grad_all[:, :, 128 * k : 128 * (k + 1)].reshape(near * rows, 128)
        part = back(left, right).astype(BF16)
        to_z = core * blocks + k
        for c in range(2):
            part_out[2 * k + c] = part[c * count : (c + 1) * count]
            stays = jnp.logical_and(to_z == z, core == c)

            @pl.when(stays)
            def _():
                part_all[z] = part_out[2 * k + c]

            @pl.when(jnp.logical_not(stays))
            def _():
                remote(
                    part_out.at[2 * k + c], part_all.at[z], part_send, part_recv,
                    {"z": to_z, "y": y, "core": c, "ch": x},
                ).start()
    keeps = core == z // blocks

    def close_parts(number):
        some = part_all.at[pl.ds(0, number)]
        copy = remote(some, some, part_send, part_recv)
        copy.wait_recv()
        copy.wait_send()

    @pl.when(keeps)
    def _():
        close_parts(zs - 1)

    @pl.when(jnp.logical_not(keeps))
    def _():
        close_parts(zs)

    w_grad[...] = sum(part_all[k].astype(F32) for k in range(zs))

    for copy in sends:
        copy.wait_send()
    remote(grad_arrivals(), grad_arrivals(), grad_send, grad_recv).wait_send()
    for into, send, recv in (
        (freq_all, freq_send, freq_recv), (sig_all, sig_send, sig_recv), (conv_all, conv_send, conv_recv)
    ):
        remote(into.at[others], into.at[others], send, recv).wait_send()


def arrived_in_order(plan, index):
    seen, done = set(), []
    for part, fz, fy, _ in plan[: index + 1]:
        if (1 - part, fz, fy) in seen and (fz, fy) != (0, 0):
            done.append((part, fz, fy))
        seen.add((part, fz, fy))
    return done


def on_device(features, w_in, short_filter, filter_spectrum, out_grad):
    zs, ys, xs = sizes = tuple(lax.axis_size(a) for a in ("z", "y", "ch"))
    rows, depth = features.shape
    piece, _, width = w_in.shape
    flat = 3 * width
    shards, near = zs * ys * 2, ys * 2
    per = width // shards
    message = (shards, per // 2, 2 * rows)
    count = out_grad.shape[1] // shards
    dma = pltpu.SemaphoreType.DMA
    vmem = pl.BlockSpec(memory_space=pltpu.VMEM)
    hbm = pl.BlockSpec(memory_space=pl.ANY)
    fixed = [jnp.asarray(t) for t in tables(shards, rows, per)]
    return pl.pallas_call(
        functools.partial(operator_kernel, sizes),
        out_shape=(
            jax.ShapeDtypeStruct((rows, width), BF16),
            jax.ShapeDtypeStruct((count, width), F32),
        ),
        in_specs=[vmem] * 3 + [hbm] * 2 + [vmem] * len(fixed),
        out_specs=(vmem, vmem),
        scratch_shapes=[
            pltpu.VMEM((rows + HALO, depth * xs), BF16),
            pltpu.VMEM((piece * shards, flat), BF16),
            pltpu.VMEM((rows + HALO, flat), F32),
            pltpu.VMEM((rows, width), F32),
            pltpu.VMEM((2, rows, width), F32),
            pltpu.VMEM((shards, 2, *message[1:]), BF16),
            pltpu.VMEM((shards, 2, *message[1:]), BF16),
            pltpu.VMEM((near, rows, zs // 2 * 128), BF16),
            *[pltpu.VMEM(message, BF16)] * 4,
            pltpu.VMEM((near, rows, width), BF16),
            pltpu.VMEM((zs, count, width), BF16),
            pltpu.VMEM((zs, count, width), BF16),
            dma((3 + zs // 2,)), dma((2, zs, ys)), dma((2, zs, ys)), dma((zs, ys)), dma((zs, ys)),
            dma((xs - 1,)), dma((xs - 1,)), dma((xs - 1,)), dma((xs - 1,)), dma, dma, dma, dma,
            dma, dma, dma((xs - 1,)), dma((xs - 1,)), dma, dma,
            dma, dma, dma((near - 1,)), dma((near - 1,)), dma, dma,
        ],
        compiler_params=pltpu.CompilerParams(
            collective_id=0, has_side_effects=True, vmem_limit_bytes=56 << 20
        ),
        name="operator",
    )(
        features, w_in.reshape(piece, flat), short_filter.reshape(3, flat),
        filter_spectrum, out_grad, *fixed,
    )


def solution(mesh):
    fine = Mesh(mesh.devices.reshape(8, 4, 2, 4), ("z", "y", "core", "ch"))
    in_specs = (
        P(CTX, "ch"),
        P(CTX, None, "ch"),
        P(None, None, "ch"),
        P(None, CTX, "ch"),
        P(CTX, None),
    )
    out_specs = (P(CTX, "ch"), P(CTX, "ch"))
    return jax.shard_map(
        on_device, mesh=fine, in_specs=in_specs, out_specs=out_specs, check_vma=False
    )
```

time: 215 us -> 125 us (0.58)
  the two profiles are of different devices: /device:TPU:2 before, /device:TPU:1 now
where the time goes in v3:
time: 125 us
  Pallas kernels  118 us (94%)
  local copies, waits for them, and re-layouts  6.16 us (5%)
    pallas_call x1, Pallas kernels, on_device(): pl.pallas_call(functools.partial(operator_kernel, sizes), out_shape=(jax....  118 us
    unnamed x3, local copies, waits for them, and re-layouts  4.54 us

profile of v3, /device:TPU:1, one launch (start us, length us, event | category | flops | bytes accessed | tf_op | source)
XLA Modules:
  0.0 125.1 jit_solution(14175506773154319026)
XLA Ops:
  0.6 1.4 %copy.18 = f32[1,3,3,512]{3,1,2,0:T(4,128)} copy(f32[1,3,3,512]{3,2,1,0:T(4,128)} %bitcast.7) | data formatting | bytes 36864
  2.0 1.6 %copy.17 = bf16[3,8,8,512]{3,2,0,1:T(8,128)(2,1)} copy(bf16[3,8,8,512]{3,2,1,0:T(8,128)(2,1)} %bitcast.5) | data formatting | bytes 393216 | tf_op jit(solution)/shard_map/reshape | solution.py:487
  3.6 118.3 %operator.1 = (bf16[192,512]{1,0:T(8,128)(2,1)}, f32[64,512]{1,0:T(8,128)}) custom-call(bf16[192,1024]{1,0:T(8,128)(2,1)} %x_in.1, bf16[64,1536]{1,0:T(8,128)(2,1)} %bitcast.4, f32[3,1536]{1,0:T(4,128)} %bitcast.6, f32[2,192,512]{2,1,0:T(8,128)} %freq_hbm.1, bf16[192,4096]{1,0:T(8,128)(2,1)} %grad_hbm.1, bf16[512,256]{1,0:T(8,128)(2,1)} %constant.16.clone.across_hi, ...), custom_call_target="tpu_custom_call" | custom-call | tf_op jit(solution)/shard_map/operator/pallas_call | solution.py:456
  121.9 1.6 %copy.21 = bf16[192,512]{1,0:T(8,128)(2,1)} copy(bf16[192,512]{1,0:T(8,128)(2,1)} %get-tuple-element.4) | data formatting | bytes 393216
  123.5 1.6 %copy.22 = f32[64,512]{1,0:T(8,128)} copy(f32[64,512]{1,0:T(8,128)} %get-tuple-element.5) | data formatting | bytes 262144

commit v4 on v3

v4 whole, which is shorter than its diff:
```python
import functools
import heapq

import jax
import jax.numpy as jnp
import numpy as np
from jax import lax
from jax.experimental import pallas as pl
from jax.experimental.pallas import tpu as pltpu
from jax.sharding import Mesh, PartitionSpec as P

CTX = ("z", "y", "core")
MESH = pl.DeviceIdType.MESH
HALO = 16
TILE = 256
MATMUL_FROM = 36
FREQ_FROM = 58
F32 = jnp.float32
BF16 = jnp.bfloat16


def ring_plan(zs, ys, share):
    z_max, z_min = zs // 2, -((zs - 1) // 2)
    y_max, y_min = ys // 2, -((ys - 1) // 2)
    size = {0: share * 2.1, 1: (1 - share) * 2.1}

    def steps(at, low, high):
        if at == 0:
            return [d for d, ok in ((1, high > 0), (-1, low < 0)) if ok]
        return [1] if 0 < at < high else [-1] if low < at < 0 else []

    def onward(part, fz, fy):
        along_z = [("z", d, (fz + d, fy)) for d in steps(fz, z_min, z_max)]
        along_y = [("y", d, (fz, fy + d)) for d in steps(fy, y_min, y_max)]
        if part == 0:
            return (along_y if fz == 0 else []) + along_z
        return (along_z if fy == 0 else []) + along_y

    free = {"y": 0.0, "z": 0.0}
    order, count = [], 2
    waiting = [(0.0, 0, 1, 0, 0), (0.0, 1, 0, 0, 0)]
    while waiting:
        now, _, part, fz, fy = heapq.heappop(waiting)
        sends = onward(part, fz, fy)
        order.append((part, fz, fy, sends))
        for axis, _, key in sends:
            free[axis] = max(free[axis], now) + size[part]
            count += 1
            heapq.heappush(waiting, (free[axis] + 1.7, count, part, *key))
    return order


def bit_reversed(count):
    bits = count.bit_length() - 1
    return np.array([int(format(i, f"0{bits}b")[::-1], 2) for i in range(count)])


def halves(table):
    high = table.astype(BF16)
    return high, (table - high.astype(np.float64)).astype(BF16)


def tables(shards, rows, per):
    total = shards * rows
    k1 = bit_reversed(shards)
    outer = 2 * np.pi / shards * (np.outer(k1, np.arange(shards)) % shards)
    turn = 2 * np.pi / total * np.outer(k1, np.arange(rows))
    turn = np.tile(np.repeat(turn, per, axis=0), (2, 1))
    inner = 2 * np.pi / rows * (np.outer(np.arange(rows), np.arange(rows)) % rows)
    across = np.kron(np.concatenate([np.cos(outer), -np.sin(outer)]), np.eye(per))
    return (
        np.stack(halves(across)),
        np.stack([np.cos(turn), np.sin(turn)]).astype(np.float32),
        np.stack([*halves(np.cos(inner)), *halves(np.sin(inner))]),
    )


def operator_kernel(
    sizes,
    x_in, w_in, taps, freq_hbm, grad_hbm, across_hbm, turn_hbm, inner_hbm,
    gated, w_grad,
    x_all, w_all, total, query, freq_in, freq_out, freq_all, freq_wide, grad_all, grad_turned,
    sig_out, sig_all, conv_out, conv_all, gated_all, part_out, part_all, across, turns, inner,
    local_sem, ring_send, ring_recv, twin_send, twin_recv, x_send, x_recv,
    halo_send, halo_recv, edge_send, edge_recv, freq_send, freq_recv,
    grad_send, grad_recv, grad_x_send, grad_x_recv, sig_send, sig_recv,
    conv_send, conv_recv, gated_send, gated_recv, part_send, part_recv,
):
    zs, ys, xs = sizes
    rows, depth = x_in.shape
    _, piece, width = w_in.shape
    flat = 3 * width
    half, quarter = width // 2, width // 4
    shards = zs * ys * 2
    near = ys * 2
    first = 5 * flat // 12 // 128 * 128
    z, y, core, x = (lax.axis_index(a) for a in ("z", "y", "core", "ch"))
    turn = 1 - 2 * core
    wrap = lambda v, n: lax.rem(v + 2 * n, n)
    here = (z * ys + y) * 2 + core
    group = y * 2 + core

    def device(place):
        return {"z": place // near, "y": place // 2 % ys, "core": place % 2, "ch": x}

    def by_axis(axis, step):
        if axis == "z":
            return {"z": wrap(z + turn * step, zs), "y": y, "core": core, "ch": x}
        if axis == "y":
            return {"z": z, "y": wrap(y + turn * step, ys), "core": core, "ch": x}
        return {"z": z, "y": y, "core": core, "ch": lax.rem(x + step, xs)}

    def in_group(other):
        return {"z": z, "y": other // 2, "core": other % 2, "ch": x}

    twin = in_group(y * 2 + 1 - core)
    after, before = lax.rem(here + 1, shards), lax.rem(here + shards - 1, shards)
    peers = [by_axis("z", 1), by_axis("z", -1), by_axis("y", 1), by_axis("y", -1), twin]
    peers += [by_axis("ch", d) for d in range(1, xs)] + [device(after), device(before)]
    barrier = pltpu.get_barrier_semaphore()
    for peer in peers:
        pl.semaphore_signal(barrier, inc=1, device_id=peer, device_id_type=MESH)

    z_low, y_low = (zs - 1) // 2, (ys - 1) // 2
    columns = (slice(0, first), slice(first, flat))

    def place_of(fz, fy, of_core):
        zo, yo = wrap(z - turn * fz, zs), wrap(y - turn * fy, ys)
        return (zo * ys + yo) * 2 + of_core

    def slot(fz, fy, of_core):
        return pl.ds(pl.multiple_of(place_of(fz, fy, of_core) * piece, piece), piece)

    def x_rows(of, n, row):
        return x_all.at[pl.ds(row, n), pl.ds(pl.multiple_of(of * depth, depth), depth)]

    share = rows // xs
    mine = pl.ds(pl.multiple_of(share * x, share), share)
    blocks = zs // 2

    def grad_piece(other, k):
        column = ((other % 2 * blocks + k) * ys + other // 2) * 128
        return grad_hbm.at[mine, pl.ds(pl.multiple_of(column, 128), 128)]

    def local(src, dst, n):
        copy = pltpu.make_async_copy(src, dst, local_sem.at[n])
        copy.start()
        return copy

    own_x = local(x_in, x_rows(x, rows, HALO), 0)
    load_freq = local(freq_hbm, freq_in, 1)
    loads = [
        local(src, dst, 2 + n)
        for n, (src, dst) in enumerate(((across_hbm, across), (turn_hbm, turns), (inner_hbm, inner)))
    ]
    loads += [
        local(grad_piece(group, k), grad_all.at[group, mine, pl.ds(128 * k, 128)], 5 + k)
        for k in range(blocks)
    ]
    for j in range(3):
        w_all[slot(0, 0, core), j * width : (j + 1) * width] = w_in[j]

    pl.semaphore_wait(barrier, len(peers))

    def remote(src, dst, send, recv, to=twin):
        return pltpu.make_async_remote_copy(
            src_ref=src, dst_ref=dst, send_sem=send, recv_sem=recv,
            device_id=to, device_id_type=MESH,
        )

    sends = []

    def start(copy):
        copy.start()
        sends.append(copy)

    def ring_copy(part, origin, key, axis, step):
        where = w_all.at[slot(*origin, core), columns[part]]
        sem = (part, key[0] + z_low, key[1] + y_low)
        return remote(where, where, ring_send.at[sem], ring_recv.at[sem], by_axis(axis, step))

    def open_x():
        start(remote(
            x_in.at[pl.ds(rows - HALO, HALO)], x_rows(x, HALO, 0), edge_send, edge_recv, device(after)
        ))
        for d in range(1, xs):
            start(remote(x_in, x_rows(x, rows, HALO), x_send.at[d - 1], x_recv.at[d - 1], by_axis("ch", d)))

    def pass_halo():
        own_x.wait()
        remote(x_in.at[pl.ds(0, HALO)], x_rows(x, HALO, 0), edge_send, edge_recv).wait_recv()
        for d in range(1, xs):
            own = x_rows(x, HALO, 0)
            start(remote(own, own, halo_send.at[d - 1], halo_recv.at[d - 1], by_axis("ch", d)))

    def close_x():
        for n, row, send, recv in ((rows, HALO, x_send, x_recv), (HALO, 0, halo_send, halo_recv)):
            for d in range(1, xs):
                theirs = x_rows(lax.rem(x + xs - d, xs), n, row)
                remote(theirs, theirs, send.at[d - 1], recv.at[d - 1]).wait_recv()

    def turn_freq():
        load_freq.wait()
        for h in range(2):
            for p in range(2):
                stacked = jnp.concatenate(
                    [freq_in[p, :, at : at + quarter] for at in (h * half, h * half + quarter)], axis=0
                )
                freq_out[:, h, p] = stacked.T.astype(BF16).reshape(shards, 2, 2 * rows)
        freq_all[here] = freq_out[here]

    later = []

    def send_freq(*key):
        later.append(key)
        if index >= FREQ_FROM:
            for each in later:
                place = place_of(*each)
                remote(freq_out.at[place], freq_all.at[here], freq_send, freq_recv, device(place)).start()
            later.clear()

    span = near * piece

    def mirror(f, n):
        return f if 2 * f == n else -f

    def meet(fz):
        for fy in range(-y_low, ys // 2 + 1):
            sem = (mirror(fz, zs) + z_low, mirror(fy, ys) + y_low)
            where = w_all.at[slot(fz, fy, 1 - core)]
            remote(where, where, twin_send.at[sem], twin_recv.at[sem]).wait_recv()
            send_freq(fz, fy, 1 - core)

    def multiply(fz, opening, tiles):
        base = pl.multiple_of(wrap(z - turn * fz, zs) * span, span)
        left = x_all[:, pl.ds(base, span)]
        begin, step, count = tiles

        @pl.loop(0, count)
        def _(n):
            cols = pl.ds(pl.multiple_of((begin + step * n) * TILE, TILE), TILE)
            part = jnp.dot(left, w_all[pl.ds(base, span), cols], preferred_element_type=F32)
            if opening:
                total[:, cols] = part
            else:
                total[:, cols] += part

    plan = ring_plan(zs, ys, first / flat)
    arrived, pending, multiplied = set(), [], []
    for index, (part, fz, fy, onward) in enumerate(plan):
        if (fz, fy) != (0, 0):
            sem = (part, fz + z_low, fy + y_low)
            where = w_all.at[slot(fz, fy, core), columns[part]]
            remote(where, where, ring_send.at[sem], ring_recv.at[sem]).wait_recv()
        for axis, step, key in onward:
            start(ring_copy(part, (fz, fy), key, axis, step))
        arrived.add((part, fz, fy))
        if (1 - part, fz, fy) in arrived:
            sem = (fz + z_low, fy + y_low)
            where = w_all.at[slot(fz, fy, core)]
            start(remote(where, where, twin_send.at[sem], twin_recv.at[sem], twin))
            if (fz, fy) != (0, 0):
                send_freq(fz, fy, core)
        if index == 1:
            open_x()
        if index == 5:
            pass_halo()
        if index == 11:
            turn_freq()
        pending += sorted(
            (k for k in range(-z_low, zs // 2 + 1) if k not in multiplied and k not in pending
             and all((p, g, f) in arrived for p in (0, 1) for g in (k, mirror(k, zs))
                     for f in range(-y_low, ys // 2 + 1))),
            key=abs,
        )
        if pending and index >= MATMUL_FROM and index % 3 == 0:
            if not multiplied:
                close_x()
            multiplied.append(pending.pop(0))
            meet(multiplied[-1])
            multiply(multiplied[-1], len(multiplied) == 1, (0, 1, flat // TILE))
    for fz in pending:
        meet(fz)

    def short(j, at):
        cols = slice(j * width + at, j * width + at + half)
        total[0:HALO, cols] = jnp.where(here == 0, 0.0, total[0:HALO, cols])
        return sum(
            taps[i, j : j + 1, at : at + half]
            * total[HALO - i : HALO - i + rows, cols].astype(BF16).astype(F32)
            for i in range(3)
        )

    def exchange(h, out, into, send, recv):
        @pl.loop(1, shards)
        def _(d):
            to = lax.rem(here + d, shards)
            remote(out.at[h, to], into.at[h, here], send.at[h], recv.at[h], device(to)).start()

        into[h, here] = out[h, here]

    others = pl.ds(0, shards - 1)

    def arrivals(h, into, send, recv):
        remote(into.at[h, others], into.at[h, others], send.at[h], recv.at[h]).wait_recv()

    for h in range(2):
        for fz in pending:
            multiply(fz, False, (2 + h, 2, 2))
        signal = short(1, h * half) * short(2, h * half)
        stacked = jnp.concatenate([signal[:, :quarter], signal[:, quarter:]], axis=0)
        sig_out[h] = stacked.T.astype(BF16).reshape(shards, 2, 2 * rows)
        exchange(h, sig_out, sig_all, sig_send, sig_recv)
    for p in range(1, near):
        other = lax.rem(group + p, near)
        for k in range(blocks):
            remote(
                grad_piece(other, k), grad_all.at[group, mine, pl.ds(128 * k, 128)],
                grad_send, grad_recv, in_group(other),
            ).start()
    for fz in pending:
        multiply(fz, False, (0, 1, 2))
    for at in (0, half):
        query[:, at : at + half] = short(0, at)
    for copy in loads:
        copy.wait()

    lines = 2 * shards
    blocks_of = (slice(0, rows), slice(rows, 2 * rows))
    mul = functools.partial(jnp.dot, preferred_element_type=F32)
    back = lambda a, b: lax.dot_general(a, b, (((0,), (0,)), ((), ())), preferred_element_type=F32)
    join = functools.partial(jnp.concatenate, axis=0)

    def split(value):
        high = value.astype(BF16)
        return high, (value - high.astype(F32)).astype(BF16)

    def within(real, imag):
        high, low = split(join([real, imag]))
        cos = mul(high, inner[0]) + mul(low, inner[0]) + mul(high, inner[1])
        sin = mul(high, inner[2]) + mul(low, inner[2]) + mul(high, inner[3])
        return cos[: 2 * lines], cos[2 * lines :], sin[: 2 * lines], sin[2 * lines :]

    def convolve(h):
        data = [sig_all[h, :, :, u].reshape(lines, rows) for u in blocks_of]
        data = [mul(across[0], d) + mul(across[1], d) for d in data]
        real, imag = join([d[:lines] for d in data]), join([d[lines:] for d in data])
        cos, sin = turns[0], turns[1]
        real_cos, imag_cos, real_sin, imag_sin = within(
            real * cos + imag * sin, imag * cos - real * sin
        )
        real, imag = real_cos + imag_sin, imag_cos - real_sin
        freq_real, freq_imag = freq_wide[h, 0], freq_wide[h, 1]
        real_cos, imag_cos, real_sin, imag_sin = within(
            real * freq_real - imag * freq_imag, real * freq_imag + imag * freq_real
        )
        real, imag = real_cos - imag_sin, imag_cos + real_sin
        real, imag = real * cos - imag * sin, imag * cos + real * sin
        for n, u in enumerate(blocks_of):
            own = slice(n * lines, (n + 1) * lines)
            high, low = split(join([real[own], imag[own]]))
            data = back(across[0], high) + back(across[0], low) + back(across[1], high)
            data = (data * (1 / (shards * rows))).astype(BF16)
            conv_out[h, :, :, u] = data.reshape(shards, 2, rows)
        exchange(h, conv_out, conv_all, conv_send, conv_recv)

    remote(freq_all.at[others], freq_all.at[others], freq_send, freq_recv).wait_recv()
    for h in range(2):
        for p in range(2):
            freq_wide[h, p] = join(
                [freq_all[:, h, p, :, u].reshape(lines, rows).astype(F32) for u in blocks_of]
            )
    for h in range(2):
        arrivals(h, sig_all, sig_send, sig_recv)
        convolve(h)

    grad_arrivals = grad_all.at[pl.ds(0, near - 1), pl.ds(0, share)]
    remote(grad_arrivals, grad_arrivals, grad_send, grad_recv).wait_recv()
    for d in range(1, xs):
        own = grad_all.at[:, mine]
        start(remote(own, own, grad_x_send.at[d - 1], grad_x_recv.at[d - 1], by_axis("ch", d)))

    def gate(h):
        arrivals(h, conv_all, conv_send, conv_recv)
        conv = conv_all[h].reshape(lines, 2 * rows).astype(F32).T
        for n in range(2):
            at = h * half + n * quarter
            value = query[:, at : at + quarter] * conv[n * rows : (n + 1) * rows]
            gated_all[h, group, :, n * quarter : (n + 1) * quarter] = value.astype(BF16)
        for p in range(1, near):
            own = gated_all.at[h, group]
            start(remote(
                own, own, gated_send.at[h, p - 1], gated_recv.at[h, p - 1],
                in_group(lax.rem(group + p, near)),
            ))
        gated[:, h * half : (h + 1) * half] = gated_all[h, group]

    for h in range(2):
        gate(h)
    for d in range(1, xs):
        of = lax.rem(x + xs - d, xs)
        theirs = grad_all.at[:, pl.ds(pl.multiple_of(share * of, share), share)]
        remote(theirs, theirs, grad_x_send.at[d - 1], grad_x_recv.at[d - 1]).wait_recv()
    grad_turned[...] = grad_all[...].reshape(near * rows, blocks * 128).T
    count = part_out.shape[2]
    for h in range(2):
        for p in range(1, near):
            theirs = gated_all.at[h, lax.rem(group + near - p, near)]
            remote(theirs, theirs, gated_send.at[h, p - 1], gated_recv.at[h, p - 1]).wait_recv()
        right = gated_all[h].reshape(near * rows, half)
        for k in range(blocks):
            part = mul(grad_turned[128 * k : 128 * (k + 1)], right).astype(BF16)
            to_z = core * blocks + k
            for c in range(2):
                part_out[h, 2 * k + c] = part[c * count : (c + 1) * count]
                stays = jnp.logical_and(to_z == z, core == c)

                @pl.when(stays)
                def _():
                    part_all[h, z] = part_out[h, 2 * k + c]

                @pl.when(jnp.logical_not(stays))
                def _():
                    remote(
                        part_out.at[h, 2 * k + c], part_all.at[h, z], part_send.at[h], part_recv.at[h],
                        {"z": to_z, "y": y, "core": c, "ch": x},
                    ).start()
    keeps = core == z // blocks

    def close_parts(h, number):
        some = part_all.at[h, pl.ds(0, number)]
        copy = remote(some, some, part_send.at[h], part_recv.at[h])
        copy.wait_recv()
        copy.wait_send()

    for h in range(2):

        @pl.when(keeps)
        def _():
            close_parts(h, zs - 1)

        @pl.when(jnp.logical_not(keeps))
        def _():
            close_parts(h, zs)

        w_grad[:, h * half : (h + 1) * half] = sum(part_all[h, k].astype(F32) for k in range(zs))

    for copy in sends:
        copy.wait_send()
    remote(grad_arrivals, grad_arrivals, grad_send, grad_recv).wait_send()
    remote(freq_all.at[others], freq_all.at[others], freq_send, freq_recv).wait_send()
    for h in range(2):
        for into, send, recv in ((sig_all, sig_send, sig_recv), (conv_all, conv_send, conv_recv)):
            remote(into.at[h, others], into.at[h, others], send.at[h], recv.at[h]).wait_send()


def settle_kernel(a, b, a_out, b_out):
    a_out[...] = a[...]
    b_out[...] = b[...]


def on_device(features, w_in, short_filter, filter_spectrum, out_grad):
    zs, ys, xs = sizes = tuple(lax.axis_size(a) for a in ("z", "y", "ch"))
    rows, depth = features.shape
    piece, _, width = w_in.shape
    flat = 3 * width
    half = width // 2
    shards, near = zs * ys * 2, ys * 2
    per = half // shards // 2
    message = (2, shards, per, 2 * rows)
    count = out_grad.shape[1] // shards
    dma = pltpu.SemaphoreType.DMA
    vmem = pl.BlockSpec(memory_space=pltpu.VMEM)
    hbm = pl.BlockSpec(memory_space=pl.ANY)
    fixed = [jnp.asarray(t) for t in tables(shards, rows, per)]
    outs = (
        jax.ShapeDtypeStruct((rows, width), BF16),
        jax.ShapeDtypeStruct((count, width), F32),
    )
    results = pl.pallas_call(
        functools.partial(operator_kernel, sizes),
        out_shape=outs,
        in_specs=[vmem] * 3 + [hbm] * 5,
        out_specs=(vmem, vmem),
        scratch_shapes=[
            pltpu.VMEM((rows + HALO, depth * xs), BF16),
            pltpu.VMEM((piece * shards, flat), BF16),
            pltpu.VMEM((rows + HALO, flat), F32),
            pltpu.VMEM((rows, width), F32),
            pltpu.VMEM((2, rows, width), F32),
            pltpu.VMEM((shards, 2, 2, per, 2 * rows), BF16),
            pltpu.VMEM((shards, 2, 2, per, 2 * rows), BF16),
            pltpu.VMEM((2, 2, 2 * per * shards, rows), F32),
            pltpu.VMEM((near, rows, zs // 2 * 128), BF16),
            pltpu.VMEM((zs // 2 * 128, near * rows), BF16),
            *[pltpu.VMEM(message, BF16)] * 4,
            pltpu.VMEM((2, near, rows, half), BF16),
            pltpu.VMEM((2, zs, count, half), BF16),
            pltpu.VMEM((2, zs, count, half), BF16),
            *[pltpu.VMEM(t.shape, t.dtype) for t in fixed],
            dma((5 + zs // 2,)), dma((2, zs, ys)), dma((2, zs, ys)), dma((zs, ys)), dma((zs, ys)),
            dma((xs - 1,)), dma((xs - 1,)), dma((xs - 1,)), dma((xs - 1,)), dma, dma, dma, dma,
            dma, dma, dma((xs - 1,)), dma((xs - 1,)), dma((2,)), dma((2,)),
            dma((2,)), dma((2,)), dma((2, near - 1)), dma((2, near - 1)), dma((2,)), dma((2,)),
        ],
        compiler_params=pltpu.CompilerParams(
            collective_id=0, has_side_effects=True, vmem_limit_bytes=56 << 20
        ),
        name="operator",
    )(features, w_in.transpose(1, 0, 2), short_filter, filter_spectrum, out_grad, *fixed)
    return pl.pallas_call(
        settle_kernel, out_shape=outs, in_specs=[vmem] * 2, out_specs=(vmem, vmem), name="settle"
    )(*results)


def solution(mesh):
    fine = Mesh(mesh.devices.reshape(8, 4, 2, 4), ("z", "y", "core", "ch"))
    in_specs = (
        P(CTX, "ch"),
        P(CTX, None, "ch"),
        P(None, None, "ch"),
        P(None, CTX, "ch"),
        P(CTX, None),
    )
    out_specs = (P(CTX, "ch"), P(CTX, "ch"))
    return jax.shard_map(
        on_device, mesh=fine, in_specs=in_specs, out_specs=out_specs, check_vma=False
    )
```

time: 125 us -> 112 us (0.90)
  Pallas kernels: 118 us -> 111 us
  local copies, waits for them, and re-layouts: 6.16 us -> 0 us
    pallas_call x1 -> x2, Pallas kernels: 118 us -> 111 us  [the longest x1 110 us: on_device(): pl.pallas_call(functools.partial(operator_kernel, sizes), out_shape=outs,...]
    unnamed x3 -> x0, local copies, waits for them, and re-layouts: 4.54 us -> none
    reshape x1 -> x0, local copies, waits for them, and re-layouts: 1.62 us -> none  [on_device(): w_in.reshape(piece, flat)]
where the time goes in v4:
time: 112 us
  Pallas kernels  111 us (99%)
    pallas_call x1, Pallas kernels, on_device(): pl.pallas_call(functools.partial(operator_kernel, sizes), out_shape=outs,...  110 us

profile of v4, /device:TPU:1, one launch (start us, length us, event | category | flops | bytes accessed | tf_op | source)
XLA Modules:
  0.0 112.0 jit_solution(15065138257602809485)
XLA Ops:
  0.6 109.6 %operator.1 = (bf16[192,512]{1,0:T(8,128)(2,1)}, f32[64,512]{1,0:T(8,128)}) custom-call(bf16[192,1024]{1,0:T(8,128)(2,1)} %x_in.1, bf16[3,64,512]{2,1,0:T(8,128)(2,1)} %bitcast.1, f32[3,3,512]{2,1,0:T(4,128)} %taps.1, f32[2,192,512]{2,1,0:T(8,128)} %freq_hbm.1, bf16[192,4096]{1,0:T(8,128)(2,1)} %grad_hbm.1, bf16[2,256,128]{2,1,0:T(8,128)(2,1)} %constant.6.clone.across_hbm, ...), custom_call_target="tpu_custom_call" | custom-call | tf_op jit(solution)/shard_map/operator/pallas_call | solution.py:480
  110.2 1.7 %settle.1 = (bf16[192,512]{1,0:T(8,128)(2,1)}, f32[64,512]{1,0:T(8,128)}) custom-call(bf16[192,512]{1,0:T(8,128)(2,1)} %get-tuple-element.4.a, f32[64,512]{1,0:T(8,128)} %get-tuple-element.5.b), custom_call_target="tpu_custom_call" | custom-call | tf_op jit(solution)/shard_map/settle/pallas_call | solution.py:511

commit v5 on v4

--- a/solution.py
+++ b/solution.py
@@ -14,7 +14,8 @@
 HALO = 16
 TILE = 256
 MATMUL_FROM = 36
-FREQ_FROM = 58
+FREQ_FROM = 11
+GRAD_AT = 1
 F32 = jnp.float32
 BF16 = jnp.bfloat16
 
@@ -77,14 +78,14 @@
 
 def operator_kernel(
     sizes,
-    x_in, w_in, taps, freq_hbm, grad_hbm, across_hbm, turn_hbm, inner_hbm,
+    x_in, w_in, taps_hbm, freq_hbm, grad_hbm, across_hbm, turn_hbm, inner_hbm,
     gated, w_grad,
     x_all, w_all, total, query, freq_in, freq_out, freq_all, freq_wide, grad_all, grad_turned,
-    sig_out, sig_all, conv_out, conv_all, gated_all, part_out, part_all, across, turns, inner,
+    sig_out, sig_all, conv_out, conv_all, gated_all, part_out, part_all, relayed, across, turns, inner, taps,
     local_sem, ring_send, ring_recv, twin_send, twin_recv, x_send, x_recv,
     halo_send, halo_recv, edge_send, edge_recv, freq_send, freq_recv,
     grad_send, grad_recv, grad_x_send, grad_x_recv, sig_send, sig_recv,
-    conv_send, conv_recv, gated_send, gated_recv, part_send, part_recv,
+    conv_send, conv_recv, gated_send, gated_recv, pair_send, pair_recv, part_send, part_recv, relay_send, relay_recv,
 ):
     zs, ys, xs = sizes
     rows, depth = x_in.shape
@@ -115,7 +116,8 @@
 
     twin = in_group(y * 2 + 1 - core)
     after, before = lax.rem(here + 1, shards), lax.rem(here + shards - 1, shards)
-    peers = [by_axis("z", 1), by_axis("z", -1), by_axis("y", 1), by_axis("y", -1), twin]
+    peers = [by_axis("z", 1), by_axis("z", -1)]
+    peers += [in_group(lax.rem(group + p, near)) for p in range(1, near)]
     peers += [by_axis("ch", d) for d in range(1, xs)] + [device(after), device(before)]
     barrier = pltpu.get_barrier_semaphore()
     for peer in peers:
@@ -147,19 +149,21 @@
         copy.start()
         return copy
 
+    own_w = [
+        local(w_in.at[j], w_all.at[slot(0, 0, core), pl.ds(j * width, width)], 6 + j) for j in range(3)
+    ]
     own_x = local(x_in, x_rows(x, rows, HALO), 0)
     load_freq = local(freq_hbm, freq_in, 1)
     loads = [
         local(src, dst, 2 + n)
-        for n, (src, dst) in enumerate(((across_hbm, across), (turn_hbm, turns), (inner_hbm, inner)))
+        for n, (src, dst) in enumerate(((across_hbm, across), (turn_hbm, turns), (inner_hbm, inner), (taps_hbm, taps)))
     ]
     loads += [
-        local(grad_piece(group, k), grad_all.at[group, mine, pl.ds(128 * k, 128)], 5 + k)
+        local(grad_piece(group, k), grad_all.at[group, mine, pl.ds(128 * k, 128)], 9 + k)
         for k in range(blocks)
     ]
-    for j in range(3):
-        w_all[slot(0, 0, core), j * width : (j + 1) * width] = w_in[j]
-
+    for copy in own_w:
+        copy.wait()
     pl.semaphore_wait(barrier, len(peers))
 
     def remote(src, dst, send, recv, to=twin):
@@ -180,15 +184,34 @@
         return remote(where, where, ring_send.at[sem], ring_recv.at[sem], by_axis(axis, step))
 
     def open_x():
+        own_x.wait()
         start(remote(
-            x_in.at[pl.ds(rows - HALO, HALO)], x_rows(x, HALO, 0), edge_send, edge_recv, device(after)
+            x_rows(x, HALO, rows), x_rows(x, HALO, 0), edge_send, edge_recv, device(after)
         ))
         for d in range(1, xs):
-            start(remote(x_in, x_rows(x, rows, HALO), x_send.at[d - 1], x_recv.at[d - 1], by_axis("ch", d)))
+            start(remote(x_rows(x, rows, HALO), x_rows(x, rows, HALO), x_send.at[d - 1], x_recv.at[d - 1], by_axis("ch", d)))
+
+    def send_grad():
+        for p in range(1, near):
+            other = lax.rem(group + p, near)
+            for k in range(blocks):
+                remote(
+                    grad_piece(other, k), grad_all.at[group, mine, pl.ds(128 * k, 128)],
+                    grad_send, grad_recv, in_group(other),
+                ).start()
+
+    grad_arrivals = grad_all.at[pl.ds(0, near - 1), pl.ds(0, share)]
+
+    def pass_grad():
+        for copy in loads:
+            copy.wait()
+        remote(grad_arrivals, grad_arrivals, grad_send, grad_recv).wait_recv()
+        for d in range(1, xs):
+            own = grad_all.at[:, mine]
+            start(remote(own, own, grad_x_send.at[d - 1], grad_x_recv.at[d - 1], by_axis("ch", d)))
 
     def pass_halo():
-        own_x.wait()
-        remote(x_in.at[pl.ds(0, HALO)], x_rows(x, HALO, 0), edge_send, edge_recv).wait_recv()
+        remote(x_rows(x, HALO, 0), x_rows(x, HALO, 0), edge_send, edge_recv).wait_recv()
         for d in range(1, xs):
             own = x_rows(x, HALO, 0)
             start(remote(own, own, halo_send.at[d - 1], halo_recv.at[d - 1], by_axis("ch", d)))
@@ -263,6 +286,8 @@
                 send_freq(fz, fy, core)
         if index == 1:
             open_x()
+        if index == GRAD_AT:
+            send_grad()
         if index == 5:
             pass_halo()
         if index == 11:
@@ -276,6 +301,7 @@
         if pending and index >= MATMUL_FROM and index % 3 == 0:
             if not multiplied:
                 close_x()
+                pass_grad()
             multiplied.append(pending.pop(0))
             meet(multiplied[-1])
             multiply(multiplied[-1], len(multiplied) == 1, (0, 1, flat // TILE))
@@ -311,19 +337,10 @@
         stacked = jnp.concatenate([signal[:, :quarter], signal[:, quarter:]], axis=0)
         sig_out[h] = stacked.T.astype(BF16).reshape(shards, 2, 2 * rows)
         exchange(h, sig_out, sig_all, sig_send, sig_recv)
-    for p in range(1, near):
-        other = lax.rem(group + p, near)
-        for k in range(blocks):
-            remote(
-                grad_piece(other, k), grad_all.at[group, mine, pl.ds(128 * k, 128)],
-                grad_send, grad_recv, in_group(other),
-            ).start()
     for fz in pending:
         multiply(fz, False, (0, 1, 2))
     for at in (0, half):
         query[:, at : at + half] = short(0, at)
-    for copy in loads:
-        copy.wait()
 
     lines = 2 * shards
     blocks_of = (slice(0, rows), slice(rows, 2 * rows))
@@ -374,11 +391,24 @@
         arrivals(h, sig_all, sig_send, sig_recv)
         convolve(h)
 
-    grad_arrivals = grad_all.at[pl.ds(0, near - 1), pl.ds(0, share)]
-    remote(grad_arrivals, grad_arrivals, grad_send, grad_recv).wait_recv()
-    for d in range(1, xs):
-        own = grad_all.at[:, mine]
-        start(remote(own, own, grad_x_send.at[d - 1], grad_x_recv.at[d - 1], by_axis("ch", d)))
+    def gated_from(h, fy, of_core):
+        return gated_all.at[h, wrap(y - turn * fy, ys) * 2 + of_core]
+
+    def pass_gated(h, fy, step):
+        block = gated_from(h, fy, core)
+        sem = (h, y_low + (ys // 2 if 2 * abs(fy + step) == ys else fy + step))
+        start(remote(block, block, gated_send.at[sem], gated_recv.at[sem], by_axis("y", step)))
+
+    def pair_gated(h, fy):
+        block, sem = gated_from(h, fy, core), (h, y_low + fy)
+        start(remote(block, block, pair_send.at[sem], pair_recv.at[sem], twin))
+
+    def take_gated(h, fy):
+        block, sem = gated_from(h, fy, core), (h, y_low + fy)
+        remote(block, block, gated_send.at[sem], gated_recv.at[sem]).wait_recv()
+        if abs(fy) == 1 and fy == 1 - 2 * h:
+            pass_gated(h, fy, fy)
+        pair_gated(h, fy)
 
     def gate(h):
         arrivals(h, conv_all, conv_send, conv_recv)
@@ -387,63 +417,125 @@
             at = h * half + n * quarter
             value = query[:, at : at + quarter] * conv[n * rows : (n + 1) * rows]
             gated_all[h, group, :, n * quarter : (n + 1) * quarter] = value.astype(BF16)
-        for p in range(1, near):
-            own = gated_all.at[h, group]
-            start(remote(
-                own, own, gated_send.at[h, p - 1], gated_recv.at[h, p - 1],
-                in_group(lax.rem(group + p, near)),
-            ))
+        pass_gated(h, 0, 1)
+        pass_gated(h, 0, -1)
+        pair_gated(h, 0)
         gated[:, h * half : (h + 1) * half] = gated_all[h, group]
 
-    for h in range(2):
-        gate(h)
     for d in range(1, xs):
         of = lax.rem(x + xs - d, xs)
         theirs = grad_all.at[:, pl.ds(pl.multiple_of(share * of, share), share)]
         remote(theirs, theirs, grad_x_send.at[d - 1], grad_x_recv.at[d - 1]).wait_recv()
     grad_turned[...] = grad_all[...].reshape(near * rows, blocks * 128).T
-    count = part_out.shape[2]
-    for h in range(2):
-        for p in range(1, near):
-            theirs = gated_all.at[h, lax.rem(group + near - p, near)]
-            remote(theirs, theirs, gated_send.at[h, p - 1], gated_recv.at[h, p - 1]).wait_recv()
+    count = w_grad.shape[0]
+
+    def distance(h, k):
+        return lax.rem((1 - 2 * h) * (z - core * blocks - k) + 2 * zs, zs)
+
+    def relay_copy(h, k, to, n):
+        step = z - (1 - 2 * h) * to
+        return remote(
+            part_out.at[h, k], relayed.at[h, n], relay_send.at[h, k], relay_recv.at[h, n],
+            {"z": wrap(step, zs), "y": y, "core": core, "ch": x},
+        )
+
+    def final_copy(h, k, c, n):
+        return remote(
+            part_out.at[h, k, pl.ds(c * count, count)], part_all.at[h, n],
+            part_send.at[h, k, c], part_recv.at[h],
+            {"z": core * blocks + k, "y": y, "core": c, "ch": x},
+        )
+
+    ends = {0: 0, 1: 1, zs - 1: 2, 2: 3, zs - 2: 4}
+    relays = {3: (1, 0), 4: (2, 1), zs - 3: (-1, 2)}
+
+    def send_part(h, k, away, act):
+        for c in range(2):
+            if away:
+                act(final_copy(h, k, c, ends[away]))
+            else:
+
+                @pl.when(core != c)
+                def _():
+                    act(final_copy(h, k, c, 0))
+
+    def products(h):
+        for fy in range(-y_low, ys // 2 + 1):
+            block, sem = gated_from(h, fy, 1 - core), (h, y_low + mirror(fy, ys))
+            remote(block, block, pair_send.at[sem], pair_recv.at[sem]).wait_recv()
         right = gated_all[h].reshape(near * rows, half)
         for k in range(blocks):
-            part = mul(grad_turned[128 * k : 128 * (k + 1)], right).astype(BF16)
-            to_z = core * blocks + k
-            for c in range(2):
-                part_out[h, 2 * k + c] = part[c * count : (c + 1) * count]
-                stays = jnp.logical_and(to_z == z, core == c)
-
-                @pl.when(stays)
+            part_out[h, k] = mul(grad_turned[128 * k : 128 * (k + 1)], right).astype(BF16)
+        for k in range(blocks):
+            for away, (to, n) in relays.items():
+
+                @pl.when(distance(h, k) == away)
                 def _():
-                    part_all[h, z] = part_out[h, 2 * k + c]
-
-                @pl.when(jnp.logical_not(stays))
+                    relay_copy(h, k, to, n).start()
+
+        for k in range(blocks):
+            for away in (1, zs - 1, 0):
+
+                @pl.when(distance(h, k) == away)
                 def _():
-                    remote(
-                        part_out.at[h, 2 * k + c], part_all.at[h, z], part_send.at[h], part_recv.at[h],
-                        {"z": to_z, "y": y, "core": c, "ch": x},
-                    ).start()
+                    send_part(h, k, away, lambda copy: copy.start())
+                    if not away:
+                        part_all[h, 0] = part_out[h, k, pl.ds(pl.multiple_of(core * count, count), count)]
+
+    def combine(h):
+        for k in range(blocks):
+            for away, inputs in ((2, (0, 1)), (zs - 2, (2,))):
+
+                @pl.when(distance(h, k) == away)
+                def _():
+                    for n in inputs:
+                        remote(
+                            relayed.at[h, n], relayed.at[h, n], relay_send.at[h, k], relay_recv.at[h, n]
+                        ).wait_recv()
+                    total_part = part_out[h, k].astype(F32)
+                    for n in inputs:
+                        total_part += relayed[h, n].astype(F32)
+                    part_out[h, k] = total_part.astype(BF16)
+                    send_part(h, k, away, lambda copy: copy.start())
+
+    gate(0)
+    take_gated(0, 1)
+    take_gated(0, -1)
+    gate(1)
+    take_gated(0, 2)
+    products(0)
+    take_gated(1, -1)
+    take_gated(1, 1)
+    combine(0)
+    take_gated(1, 2)
+    products(1)
+    combine(1)
     keeps = core == z // blocks
 
     def close_parts(h, number):
         some = part_all.at[h, pl.ds(0, number)]
-        copy = remote(some, some, part_send.at[h], part_recv.at[h])
-        copy.wait_recv()
-        copy.wait_send()
+        remote(some, some, part_send.at[h, 0, 0], part_recv.at[h]).wait_recv()
 
     for h in range(2):
 
         @pl.when(keeps)
         def _():
-            close_parts(h, zs - 1)
+            close_parts(h, len(ends) - 1)
 
         @pl.when(jnp.logical_not(keeps))
         def _():
-            close_parts(h, zs)
-
-        w_grad[:, h * half : (h + 1) * half] = sum(part_all[h, k].astype(F32) for k in range(zs))
+            close_parts(h, len(ends))
+
+        w_grad[:, h * half : (h + 1) * half] = sum(part_all[h, n].astype(F32) for n in range(len(ends)))
+        for k in range(blocks):
+            for away in range(zs):
+
+                @pl.when(distance(h, k) == away)
+                def _():
+                    if away in relays:
+                        relay_copy(h, k, *relays[away]).wait_send()
+                    else:
+                        send_part(h, k, away, lambda copy: copy.wait_send())
 
     for copy in sends:
         copy.wait_send()
@@ -480,7 +572,7 @@
     results = pl.pallas_call(
         functools.partial(operator_kernel, sizes),
         out_shape=outs,
-        in_specs=[vmem] * 3 + [hbm] * 5,
+        in_specs=[hbm] * 8,
         out_specs=(vmem, vmem),
         scratch_shapes=[
             pltpu.VMEM((rows + HALO, depth * xs), BF16),
@@ -495,13 +587,16 @@
             pltpu.VMEM((zs // 2 * 128, near * rows), BF16),
             *[pltpu.VMEM(message, BF16)] * 4,
             pltpu.VMEM((2, near, rows, half), BF16),
-            pltpu.VMEM((2, zs, count, half), BF16),
-            pltpu.VMEM((2, zs, count, half), BF16),
+            pltpu.VMEM((2, zs // 2, 2 * count, half), BF16),
+            pltpu.VMEM((2, 5, count, half), BF16),
+            pltpu.VMEM((2, 3, 2 * count, half), BF16),
             *[pltpu.VMEM(t.shape, t.dtype) for t in fixed],
-            dma((5 + zs // 2,)), dma((2, zs, ys)), dma((2, zs, ys)), dma((zs, ys)), dma((zs, ys)),
+            pltpu.VMEM(short_filter.shape, F32),
+            dma((9 + zs // 2,)), dma((2, zs, ys)), dma((2, zs, ys)), dma((zs, ys)), dma((zs, ys)),
             dma((xs - 1,)), dma((xs - 1,)), dma((xs - 1,)), dma((xs - 1,)), dma, dma, dma, dma,
             dma, dma, dma((xs - 1,)), dma((xs - 1,)), dma((2,)), dma((2,)),
-            dma((2,)), dma((2,)), dma((2, near - 1)), dma((2, near - 1)), dma((2,)), dma((2,)),
+            dma((2,)), dma((2,)), dma((2, ys)), dma((2, ys)), dma((2, ys)), dma((2, ys)), dma((2, zs // 2, 2)), dma((2,)),
+            dma((2, zs // 2)), dma((2, 3)),
         ],
         compiler_params=pltpu.CompilerParams(
             collective_id=0, has_side_effects=True, vmem_limit_bytes=56 << 20

time: 112 us -> 104 us (0.929)
  Pallas kernels: 111 us -> 103 us
    pallas_call x1, Pallas kernels: 110 us -> 102 us  [on_device(): pl.pallas_call(functools.partial(operator_kernel, sizes), out_shape=outs,...]
where the time goes in v5:
time: 104 us
  Pallas kernels  103 us (99%)
    pallas_call x1, Pallas kernels, on_device(): pl.pallas_call(functools.partial(operator_kernel, sizes), out_shape=outs,...  102 us

profile of v5, /device:TPU:1, one launch (start us, length us, event | category | flops | bytes accessed | tf_op | source)
XLA Modules:
  0.0 104.1 jit_solution(1601367923352156789)
XLA Ops:
  0.6 101.7 %operator.1 = (bf16[192,512]{1,0:T(8,128)(2,1)}, f32[64,512]{1,0:T(8,128)}) custom-call(bf16[192,1024]{1,0:T(8,128)(2,1)} %x_in.1, bf16[3,64,512]{2,1,0:T(8,128)(2,1)} %bitcast.1, f32[3,3,512]{2,1,0:T(4,128)} %taps_hbm.1, f32[2,192,512]{2,1,0:T(8,128)} %freq_hbm.1, bf16[192,4096]{1,0:T(8,128)(2,1)} %grad_hbm.1, ...), custom_call_target="tpu_custom_call" | custom-call | tf_op jit(solution)/shard_map/operator/pallas_call | solution.py:572
  102.4 1.7 %settle.1 = (bf16[192,512]{1,0:T(8,128)(2,1)}, f32[64,512]{1,0:T(8,128)}) custom-call(bf16[192,512]{1,0:T(8,128)(2,1)} %get-tuple-element.4.a, f32[64,512]{1,0:T(8,128)} %get-tuple-element.5.b), custom_call_target="tpu_custom_call" | custom-call | tf_op jit(solution)/shard_map/settle/pallas_call | solution.py:606

commit v6 on v5

--- a/solution.py
+++ b/solution.py
@@ -102,7 +102,8 @@
     group = y * 2 + core
 
     def device(place):
-        return {"z": place // near, "y": place // 2 % ys, "core": place % 2, "ch": x}
+        chip = lax.div(place, 2)
+        return {"z": lax.div(chip, ys), "y": lax.rem(chip, ys), "core": lax.rem(place, 2), "ch": x}
 
     def by_axis(axis, step):
         if axis == "z":
@@ -318,9 +319,9 @@
         )
 
     def exchange(h, out, into, send, recv):
-        @pl.loop(1, shards)
-        def _(d):
-            to = lax.rem(here + d, shards)
+        @pl.loop(0, shards - 1)
+        def _(n):
+            to = lax.rem(here + 1 + n, shards)
             remote(out.at[h, to], into.at[h, here], send.at[h], recv.at[h], device(to)).start()
 
         into[h, here] = out[h, here]

time: 104 us -> 105 us (level)
  no operation moved by 1% of the time
where the time goes in v6:
time: 105 us
  Pallas kernels  104 us (99%)
    pallas_call x1, Pallas kernels, on_device(): pl.pallas_call(functools.partial(operator_kernel, sizes), out_shape=outs,...  102 us

profile of v6, /device:TPU:1, one launch (start us, length us, event | category | flops | bytes accessed | tf_op | source)
XLA Modules:
  0.0 104.5 jit_solution(10745063155893385713)
XLA Ops:
  0.6 102.2 %operator.1 = (bf16[192,512]{1,0:T(8,128)(2,1)}, f32[64,512]{1,0:T(8,128)}) custom-call(bf16[192,1024]{1,0:T(8,128)(2,1)} %x_in.1, bf16[3,64,512]{2,1,0:T(8,128)(2,1)} %bitcast.1, f32[3,3,512]{2,1,0:T(4,128)} %taps_hbm.1, f32[2,192,512]{2,1,0:T(8,128)} %freq_hbm.1, bf16[192,4096]{1,0:T(8,128)(2,1)} %grad_hbm.1, ...), custom_call_target="tpu_custom_call" | custom-call | tf_op jit(solution)/shard_map/operator/pallas_call | solution.py:573
  102.8 1.7 %settle.1 = (bf16[192,512]{1,0:T(8,128)(2,1)}, f32[64,512]{1,0:T(8,128)}) custom-call(bf16[192,512]{1,0:T(8,128)(2,1)} %get-tuple-element.4.a, f32[64,512]{1,0:T(8,128)} %get-tuple-element.5.b), custom_call_target="tpu_custom_call" | custom-call | tf_op jit(solution)/shard_map/settle/pallas_call | solution.py:607

commit v7 on v6

--- a/solution.py
+++ b/solution.py
@@ -500,16 +500,16 @@
                     send_part(h, k, away, lambda copy: copy.start())
 
     gate(0)
+    gate(1)
     take_gated(0, 1)
+    take_gated(1, -1)
     take_gated(0, -1)
-    gate(1)
+    take_gated(1, 1)
     take_gated(0, 2)
     products(0)
-    take_gated(1, -1)
-    take_gated(1, 1)
-    combine(0)
     take_gated(1, 2)
     products(1)
+    combine(0)
     combine(1)
     keeps = core == z // blocks
 

time: 105 us -> 103 us (0.981)
  Pallas kernels: 104 us -> 102 us
    pallas_call x1, Pallas kernels: 102 us -> 100 us  [on_device(): pl.pallas_call(functools.partial(operator_kernel, sizes), out_shape=outs,...]
where the time goes in v7:
time: 103 us
  Pallas kernels  102 us (99%)
    pallas_call x1, Pallas kernels, on_device(): pl.pallas_call(functools.partial(operator_kernel, sizes), out_shape=outs,...  100 us

profile of v7, /device:TPU:1, one launch (start us, length us, event | category | flops | bytes accessed | tf_op | source)
XLA Modules:
  0.0 102.7 jit_solution(8190742834506689913)
XLA Ops:
  0.6 100.4 %operator.1 = (bf16[192,512]{1,0:T(8,128)(2,1)}, f32[64,512]{1,0:T(8,128)}) custom-call(bf16[192,1024]{1,0:T(8,128)(2,1)} %x_in.1, bf16[3,64,512]{2,1,0:T(8,128)(2,1)} %bitcast.1, f32[3,3,512]{2,1,0:T(4,128)} %taps_hbm.1, f32[2,192,512]{2,1,0:T(8,128)} %freq_hbm.1, bf16[192,4096]{1,0:T(8,128)(2,1)} %grad_hbm.1, ...), custom_call_target="tpu_custom_call" | custom-call | tf_op jit(solution)/shard_map/operator/pallas_call | solution.py:573
  101.0 1.7 %settle.1 = (bf16[192,512]{1,0:T(8,128)(2,1)}, f32[64,512]{1,0:T(8,128)}) custom-call(bf16[192,512]{1,0:T(8,128)(2,1)} %get-tuple-element.4.a, f32[64,512]{1,0:T(8,128)} %get-tuple-element.5.b), custom_call_target="tpu_custom_call" | custom-call | tf_op jit(solution)/shard_map/settle/pallas_call | solution.py:607

commit v8 on v7

--- a/solution.py
+++ b/solution.py
@@ -382,6 +382,11 @@
             conv_out[h, :, :, u] = data.reshape(shards, 2, rows)
         exchange(h, conv_out, conv_all, conv_send, conv_recv)
 
+    for d in range(1, xs):
+        of = lax.rem(x + xs - d, xs)
+        theirs = grad_all.at[:, pl.ds(pl.multiple_of(share * of, share), share)]
+        remote(theirs, theirs, grad_x_send.at[d - 1], grad_x_recv.at[d - 1]).wait_recv()
+    grad_turned[...] = grad_all[...].reshape(near * rows, blocks * 128).T
     remote(freq_all.at[others], freq_all.at[others], freq_send, freq_recv).wait_recv()
     for h in range(2):
         for p in range(2):
@@ -423,11 +428,6 @@
         pair_gated(h, 0)
         gated[:, h * half : (h + 1) * half] = gated_all[h, group]
 
-    for d in range(1, xs):
-        of = lax.rem(x + xs - d, xs)
-        theirs = grad_all.at[:, pl.ds(pl.multiple_of(share * of, share), share)]
-        remote(theirs, theirs, grad_x_send.at[d - 1], grad_x_recv.at[d - 1]).wait_recv()
-    grad_turned[...] = grad_all[...].reshape(near * rows, blocks * 128).T
     count = w_grad.shape[0]
 
     def distance(h, k):
@@ -467,14 +467,12 @@
         right = gated_all[h].reshape(near * rows, half)
         for k in range(blocks):
             part_out[h, k] = mul(grad_turned[128 * k : 128 * (k + 1)], right).astype(BF16)
-        for k in range(blocks):
             for away, (to, n) in relays.items():
 
                 @pl.when(distance(h, k) == away)
                 def _():
                     relay_copy(h, k, to, n).start()
 
-        for k in range(blocks):
             for away in (1, zs - 1, 0):
 
                 @pl.when(distance(h, k) == away)

time: 103 us -> 104 us (level)
  no operation moved by 1% of the time
where the time goes in v8:
time: 104 us
  Pallas kernels  103 us (99%)
    pallas_call x1, Pallas kernels, on_device(): pl.pallas_call(functools.partial(operator_kernel, sizes), out_shape=outs,...  101 us

profile of v8, /device:TPU:1, one launch (start us, length us, event | category | flops | bytes accessed | tf_op | source)
XLA Modules:
  0.0 103.5 jit_solution(3665453591404778181)
XLA Ops:
  0.6 101.1 %operator.1 = (bf16[192,512]{1,0:T(8,128)(2,1)}, f32[64,512]{1,0:T(8,128)}) custom-call(bf16[192,1024]{1,0:T(8,128)(2,1)} %x_in.1, bf16[3,64,512]{2,1,0:T(8,128)(2,1)} %bitcast.1, f32[3,3,512]{2,1,0:T(4,128)} %taps_hbm.1, f32[2,192,512]{2,1,0:T(8,128)} %freq_hbm.1, bf16[192,4096]{1,0:T(8,128)(2,1)} %grad_hbm.1, ...), custom_call_target="tpu_custom_call" | custom-call | tf_op jit(solution)/shard_map/operator/pallas_call | solution.py:571
  101.8 1.7 %settle.1 = (bf16[192,512]{1,0:T(8,128)(2,1)}, f32[64,512]{1,0:T(8,128)}) custom-call(bf16[192,512]{1,0:T(8,128)(2,1)} %get-tuple-element.4.a, f32[64,512]{1,0:T(8,128)} %get-tuple-element.5.b), custom_call_target="tpu_custom_call" | custom-call | tf_op jit(solution)/shard_map/settle/pallas_call | solution.py:605
